TPU v7x, 32 devices: a whole 2x2x4 slice. The times are simulated.
32 devices in a mesh: grp: 2 (over x), wide: 16 (over z, y, core).
Axes of the slice: x: 2, y: 2, z: 4, core: 2. Of those that a mesh axis runs over, the one named last changes fastest.
Arguments:
- raw: bfloat16 [4096, 16, 2048], P(('grp', 'wide')), parts along dimension 0, may hold values from -6 to 6
- cell_feed: int32 [1024], replicated, may hold values from 0 to 1023, each once
- dm_delay: int32 [1024, 1024], replicated, may hold values from 0 to 15
Outputs:
- dedispersed: float32 [2048, 16, 1024], P(('grp', 'wide')), parts along dimension 0
There are 2 independent parts, one for each index of `grp`. A program takes and returns all parts, laid end to end along the dimension named above; an argument that names none is the same for every part. Nothing has to cross between parts.
Inputs may be any that keep to these rules, and one draw needn't show every extreme that they name: `cell_feed`: every antenna stands at exactly one cell.
All inputs are finite; a program needn't handle non-finite values.
Results may differ from a plain program's by a relative error of at most 0.0084.
Values may be sent and summed in bfloat16 or wider, within the bound.
No kernel may reach another device: no remote copies, remote signals or barrier semaphores. Data moves between devices by JAX's collectives and lax.ppermute only.
A program may use at most 128 MiB of HBM per device.

v0:
```python
import functools
import math

import jax
import jax.numpy as jnp
import numpy as np
from jax import lax
from jax.experimental import pallas as pl
from jax.experimental.pallas import tpu as pltpu
from jax.sharding import PartitionSpec as P


LANES = 128
VMEM_LIMIT = 58 * 1024 * 1024

EAST_COSINE = np.array([[1, 1, 1, 1], [1, 0, -1, 0], [1, -1, 1, -1], [1, 0, -1, 0]], np.float32)
EAST_SINE = np.array([[0, 0, 0, 0], [0, 1, 0, -1], [0, 0, 0, 0], [0, -1, 0, 1]], np.float32)


def phase_pair(count, length):
    angle = (count % length).astype(jnp.float32) * (2.0 * math.pi / length)
    return (jnp.cos(angle), jnp.sin(angle))


def channel_table(samples, width):
    sample_ids = lax.broadcasted_iota(jnp.int32, (samples, width), 0)
    freq_ids = lax.broadcasted_iota(jnp.int32, (samples, width), 1)
    cosine, sine = phase_pair(sample_ids * freq_ids, samples)
    factor = 1.0 / math.sqrt(samples)
    return jnp.concatenate([cosine * factor, -sine * factor], axis=1).astype(jnp.bfloat16)


def sky_table(cells):
    rows = lax.broadcasted_iota(jnp.int32, (cells, cells), 0)
    cols = lax.broadcasted_iota(jnp.int32, (cells, cells), 1)
    cosine, sine = phase_pair(rows * cols, cells)
    real_row = jnp.stack([cosine, sine], axis=-1)
    imag_row = jnp.stack([-sine, cosine], axis=-1)
    factor = 1.0 / math.sqrt(cells)
    return (jnp.stack([real_row, imag_row], axis=1) * factor).astype(jnp.bfloat16)


def transform_table(frames):
    terms = frames // 2 + 1
    harmonic = lax.broadcasted_iota(jnp.int32, (terms, frames), 0)
    moment = lax.broadcasted_iota(jnp.int32, (terms, frames), 1)
    cosine, sine = phase_pair(harmonic * moment, frames)
    return jnp.stack([cosine, -sine]).astype(jnp.bfloat16)


def beam_power(spec, feed_index, table):
    grid = jnp.take(spec, feed_index.reshape(-1), axis=0)
    grid = grid.reshape(feed_index.shape + spec.shape[1:])
    beams = jnp.einsum("joni,penrif->poerfj", table, grid, preferred_element_type=jnp.float32)
    real_part = beams[:, 0]
    imag_part = beams[:, 1]
    cosines = jnp.asarray(EAST_COSINE)
    sines = jnp.asarray(EAST_SINE)
    high = lax.Precision.HIGHEST
    east_real = 0.5 * (
        jnp.einsum("qe,perfj->prfqj", cosines, real_part, precision=high)
        + jnp.einsum("qe,perfj->prfqj", sines, imag_part, precision=high)
    )
    east_imag = 0.5 * (
        jnp.einsum("qe,perfj->prfqj", cosines, imag_part, precision=high)
        - jnp.einsum("qe,perfj->prfqj", sines, real_part, precision=high)
    )
    power = 0.5 * jnp.sum(east_real * east_real + east_imag * east_imag, axis=0)
    return power.reshape(power.shape[0], power.shape[1], -1)


def dedisperse(spectrum, dm_delay, frames):
    base_cos, base_sin = phase_pair(jnp.transpose(dm_delay), frames)
    beams_dev = spectrum.shape[3]
    nfreq = spectrum.shape[2]

    def one_term(carry, block):
        cosine, sine = carry
        cos_half = cosine.astype(jnp.bfloat16)
        sin_half = sine.astype(jnp.bfloat16)
        upper = jnp.concatenate([cos_half, sin_half], axis=1)
        lower = jnp.concatenate([-sin_half, cos_half], axis=1)
        right = jnp.concatenate([upper, lower], axis=0)
        left = block.reshape(2 * nfreq, beams_dev)
        result = lax.dot_general(
            left, right, (((0,), (0,)), ((), ())), preferred_element_type=jnp.float32
        )
        next_cos = cosine * base_cos - sine * base_sin
        next_sin = sine * base_cos + cosine * base_sin
        return ((next_cos, next_sin), result)

    start = (jnp.ones(base_cos.shape, jnp.float32), jnp.zeros(base_cos.shape, jnp.float32))
    _, trials = lax.scan(one_term, start, spectrum)
    return trials.reshape(trials.shape[0], beams_dev, 2, -1)


def synthesis(trials, frames, nfreq):
    terms = frames // 2 + 1
    moment = lax.broadcasted_iota(jnp.int32, (frames, terms), 0)
    harmonic = lax.broadcasted_iota(jnp.int32, (frames, terms), 1)
    cosine, sine = phase_pair(moment * harmonic, frames)
    weight = jnp.where((harmonic == 0) | (harmonic * 2 == frames), 1.0, 2.0).astype(jnp.float32)
    weight = weight / (frames * math.sqrt(nfreq))
    table = jnp.stack([cosine * weight, -sine * weight], axis=1)
    return jnp.einsum("tuk,kbud->btd", table, trials, precision=lax.Precision.HIGHEST)


def plain_body(raw, cell_feed, dm_delay):
    feed_dev, frames, samples = raw.shape
    nfreq = samples // 2
    table = channel_table(samples, nfreq)
    spectra = jnp.dot(
        raw.reshape(feed_dev * frames, samples), table, preferred_element_type=jnp.float32
    )
    spectra = spectra.astype(jnp.bfloat16).reshape(feed_dev, frames, 2, nfreq)
    cells = cell_feed.shape[0] // 4
    polar = lax.broadcasted_iota(jnp.int32, (2, 4, cells), 0)
    feed_index = 2 * cell_feed.reshape(1, 4, cells) + polar
    table_sky = sky_table(cells)
    arrived = lax.all_to_all(spectra, "wide", split_axis=3, concat_axis=0, tiled=True)
    power = beam_power(arrived, feed_index, table_sky)
    centred = (power - jnp.mean(power, axis=0, keepdims=True)).astype(jnp.bfloat16)
    time_table = transform_table(frames)
    local = jnp.einsum("okr,rfb->kofb", time_table, centred, preferred_element_type=jnp.float32)
    spectrum = lax.all_to_all(
        local.astype(jnp.bfloat16), "wide", split_axis=3, concat_axis=2, tiled=True
    )
    trials = dedisperse(spectrum, dm_delay, frames)
    return synthesis(trials, frames, nfreq)


def params(steps=1):
    return pltpu.CompilerParams(
        dimension_semantics=("arbitrary",) * steps, vmem_limit_bytes=VMEM_LIMIT
    )


def cost(flops, nbytes):
    return pl.CostEstimate(flops=int(flops), bytes_accessed=int(nbytes), transcendentals=0)


def angle_tables(samples, parts, kdev, low):
    freq = np.arange(parts)[:, None] * kdev + np.tile(np.arange(kdev), 2)[None, :]
    quarter = np.repeat(np.arange(2), kdev) * (samples // 4)
    coarse = np.arange(0, samples, low)[None, :, None] * freq[:, None, :] % samples
    fine = (np.arange(low)[None, :, None] * freq[:, None, :] + quarter) % samples
    turn = 2.0 * np.pi / samples
    factor = 1.0 / math.sqrt(samples)
    first = np.stack([np.cos(coarse * turn), np.sin(coarse * turn)])
    second = np.stack([np.cos(fine * turn), np.sin(fine * turn)]) * factor
    return first.astype(np.float32), second.astype(np.float32)


def channelise_kernel(low, begin, frames, me_ref, coarse_ref, fine_ref, raw_ref, *refs):
    split = len(refs) > 4
    out_refs = refs[:-4] if split else refs[:1]
    table, rows, order = refs[-4:-1] if split else refs[1:]
    out_ref = refs[-1] if split else refs[0]
    _, samples, _ = table.shape
    parts, count, pols, antennas, lanes = out_ref.shape
    own = order.shape[0]
    steps = rows.shape[0] // own
    group = antennas // steps
    pairs = parts // 2
    step = pl.program_id(0)

    def make(pair, slot):
        for side in range(2):
            part = 2 * pair + side
            fine_cos, fine_sin = fine_ref[0, part], fine_ref[1, part]
            for block in range(samples // low):
                cos_a = coarse_ref[0, part, block : block + 1, :]
                sin_a = coarse_ref[1, part, block : block + 1, :]
                value = cos_a * fine_cos - sin_a * fine_sin
                table[slot, block * low : (block + 1) * low, side * lanes : (side + 1) * lanes] = (
                    value.astype(jnp.bfloat16)
                )

    @pl.when(step == 0)
    def _():
        line = lax.broadcasted_iota(jnp.int32, order.shape, 0)
        column = lax.broadcasted_iota(jnp.int32, order.shape, 1)
        bits, pol_bits = group.bit_length() - 1, pols.bit_length() - 1
        antenna, pol = line & (group - 1), (line >> bits) & (pols - 1)
        wanted = (antenna * pols + pol) * frames + begin + (line >> (bits + pol_bits))
        order[...] = jnp.where(wanted == column, 1.0, 0.0).astype(jnp.bfloat16)
        make(0, 0)

    source = raw_ref[...].reshape(-1, samples)
    ordered = jnp.dot(order[...], source, preferred_element_type=jnp.float32)
    rows[pl.ds(pl.multiple_of(step * own, own), own), :] = ordered.astype(jnp.bfloat16)

    def use(pair, slot):
        value = jnp.dot(rows[...], table[slot], preferred_element_type=jnp.float32)
        value = value.astype(jnp.bfloat16)
        for side in range(2):
            for i in range(steps):
                block = value[i * own : (i + 1) * own, side * lanes : (side + 1) * lanes]
                out_ref[2 * pair + side, :, :, i * group : (i + 1) * group, :] = block.reshape(
                    count, pols, group, lanes
                )

    @pl.when(step == steps - 1)
    def _():
        def one(twice, carry):
            for slot in range(2):
                pair = 2 * twice + slot
                make(lax.rem(pair + 1, pairs), 1 - slot)
                use(pair, slot)
            return carry

        lax.fori_loop(0, pairs // 2, one, 0)
        if split:
            for part in range(parts):
                out_refs[part][...] = out_ref[lax.rem(me_ref[0] + part, parts)]


def channelise(raw, me, first, count, parts, split):
    feed_dev, frames, samples = raw.shape
    kdev = samples // 2 // parts
    low = 64
    group = 16
    steps = feed_dev // (2 * group)
    coarse, fine = angle_tables(samples, parts, kdev, low)
    own = 2 * group * count
    piece = (count, 2, feed_dev // 2, LANES)
    shapes = [piece] * parts if split else [(parts, *piece)]
    whole = lambda shape: pl.BlockSpec(shape, lambda i, me_ref: (0,) * len(shape))
    scratch = [
        pltpu.VMEM((2, samples, 2 * LANES), jnp.bfloat16),
        pltpu.VMEM((steps * own, samples), jnp.bfloat16),
        pltpu.VMEM((own, 2 * group * frames), jnp.bfloat16),
    ]
    if split:
        scratch.append(pltpu.VMEM((parts, *piece), jnp.bfloat16))
    result = pl.pallas_call(
        functools.partial(channelise_kernel, low, first, frames),
        name="channelise",
        grid_spec=pltpu.PrefetchScalarGridSpec(
            num_scalar_prefetch=1,
            grid=(steps,),
            in_specs=[
                whole(coarse.shape),
                whole(fine.shape),
                pl.BlockSpec((2 * group, frames, samples), lambda i, me_ref: (i, 0, 0)),
            ],
            out_specs=[whole(shape) for shape in shapes],
            scratch_shapes=scratch,
        ),
        out_shape=[jax.ShapeDtypeStruct(shape, jnp.bfloat16) for shape in shapes],
        compiler_params=params(),
        cost_estimate=cost(
            2 * feed_dev * count * samples * samples, 4 * raw.size
        ),
    )(me, jnp.asarray(coarse), jnp.asarray(fine), raw)
    return result if split else result[0]


def beam_table(cell_feed, me, parts):
    beams = cell_feed.shape[0]
    cells = beams // 4
    own = beams // parts
    antenna = lax.broadcasted_iota(jnp.int32, (beams, beams), 0)
    cell = lax.broadcasted_iota(jnp.int32, (beams, beams), 1)
    antenna = (me - antenna // own + parts) % parts * own + antenna % own
    place = jnp.sum(jnp.where(cell_feed[None, :] == antenna, cell, 0), axis=1)
    east, north = place // cells, place % cells
    count = lax.broadcasted_iota(jnp.int32, (cells, beams), 0) * north[None, :]
    cosine, sine = phase_pair(count, cells)
    factor = 1.0 / math.sqrt(cells)
    cosine = (cosine * factor).astype(jnp.bfloat16)
    sine = (sine * factor).astype(jnp.bfloat16)
    cosine, sine = lax.optimization_barrier((cosine, sine))
    quarters = jnp.arange(4, dtype=jnp.int32)[:, None, None] * east % 4
    odd, minus = quarters % 2 == 1, quarters >= 2
    real = jnp.where(odd, -sine, cosine)
    imag = jnp.where(odd, -cosine, -sine)
    table = jnp.stack([jnp.where(minus, -real, real), jnp.where(minus, -imag, imag)])
    order = (me + jnp.arange(parts, dtype=jnp.int32)) % parts
    return jnp.take(table.reshape(2, parts, own, beams), order, axis=1).reshape(2, beams, beams)


def beam_kernel(frames, n_spec, n_prev, me_ref, weight_ref, *refs):
    spec_refs, prev_refs = refs[:n_spec], refs[n_spec : n_spec + n_prev]
    out_refs, right = refs[n_spec + n_prev : -1], refs[-1]
    last = len(out_refs) > 1
    count, pols, group, lanes = spec_refs[0].shape[-4:]
    tile = weight_ref.shape[1]
    parts = weight_ref.shape[2] // group
    half = lanes // 2
    pairs = count // 2

    @pl.when(pl.program_id(0) == 0)
    def _():
        for d in range(parts):
            for r in range(count):
                for p in range(pols):
                    at = (r % 2 * pols + p) * lanes
                    if n_spec == 1:
                        block = spec_refs[0][lax.rem(me_ref[0] + (parts - d), parts), r, p]
                    else:
                        block = spec_refs[d][r, p]
                    right[r // 2, d * group : (d + 1) * group, at : at + lanes] = block

    low = lax.broadcasted_iota(jnp.int32, (tile, lanes), 1) < half
    sign = jnp.where(low, -1.0, 1.0)

    def power_of(pair):
        first = jnp.dot(weight_ref[0], right[pair], preferred_element_type=jnp.float32)
        second = jnp.dot(weight_ref[1], right[pair], preferred_element_type=jnp.float32)
        sums = []
        for r in range(2):
            total = None
            for p in range(pols):
                cut = slice((r * pols + p) * lanes, (r * pols + p + 1) * lanes)
                turned = pltpu.roll(second[:, cut], half, 1)
                value = first[:, cut] + sign * turned
                total = value * value if total is None else total + value * value
            sums.append(0.125 * (total + pltpu.roll(total, half, 1)))
        return jnp.where(low, sums[0], sums[1])

    if not last:

        def one(pair, carry):
            out_refs[0][pair] = power_of(pair)
            return carry

        lax.fori_loop(0, pairs, one, 0)

    if last:
        powers = [power_of(pair) for pair in range(pairs)]
        blocks = [ref[i] for ref in prev_refs for i in range(ref.shape[0])] + powers
        total = functools.reduce(lambda a, b: a + b, blocks)
        mean = (total + pltpu.roll(total, half, 1)) * (1.0 / frames)
        hold = out_refs[-1]
        own = hold.shape[2]
        per = tile // own
        at = pl.program_id(0) * per
        for i, block in enumerate(blocks):
            hold[pl.ds(at, per), i] = (block - mean).astype(jnp.bfloat16).reshape(per, own, lanes)

        @pl.when(pl.program_id(0) == pl.num_programs(0) - 1)
        def _():
            for part in range(hold.shape[0]):
                out_refs[part][...] = hold[part]


def beam_stage(weights, me, arrived, frames, parts, prev=None, share=(0, 1)):
    count, pols, group, lanes = arrived[0].shape[-4:]
    beams = weights.shape[1]
    tile = 256
    whole = lambda shape: pl.BlockSpec(shape, lambda i, me_ref: (0,) * len(shape))
    steps = beams // tile // share[1]
    begin = steps * share[0]
    rows = lambda power: pl.BlockSpec(
        (power.shape[0], tile, lanes), lambda i, me_ref: (0, begin + i, 0)
    )
    scratch = [pltpu.VMEM((count // 2, parts * group, 2 * pols * lanes), jnp.bfloat16)]
    before = prev or []
    if prev is None:
        out_shape = [jax.ShapeDtypeStruct((count // 2, beams, lanes), jnp.float32)]
        out_specs = [rows(out_shape[0])]
    else:
        piece = (frames // 2, beams // parts, lanes)
        out_shape = [jax.ShapeDtypeStruct(piece, jnp.bfloat16)] * (parts // share[1])
        out_specs = [whole(piece)] * (parts // share[1])
        scratch.insert(0, pltpu.VMEM((parts // share[1], *piece), jnp.bfloat16))
    result = pl.pallas_call(
        functools.partial(beam_kernel, frames, len(arrived), len(before)),
        name="beams",
        grid_spec=pltpu.PrefetchScalarGridSpec(
            num_scalar_prefetch=1,
            grid=(steps,),
            in_specs=[pl.BlockSpec((2, tile, beams), lambda i, me_ref: (0, begin + i, 0))]
            + [whole(piece.shape) for piece in arrived]
            + [rows(power) for power in before],
            out_specs=out_specs,
            scratch_shapes=scratch,
        ),
        out_shape=out_shape,
        compiler_params=params(),
        cost_estimate=cost(
            4 * beams * beams * count * pols * lanes // share[1],
            4 * weights.size + 4 * beams * count * lanes,
        ),
    )(me, weights, *arrived, *before)
    return result[0] if prev is None else result


def turn_value(count, frames):
    folded = jnp.minimum(count, frames - count)
    inner = jnp.minimum(folded, frames // 2 - folded)
    value = jnp.zeros(count.shape, jnp.float32)
    for i in range(frames // 4):
        value = jnp.where(inner == i, np.float32(math.cos(2.0 * math.pi * i / frames)), value)
    return jnp.where(folded > frames // 4, -value, value)


def factor_kernel(frames, delay_ref, out_ref):
    delay = delay_ref[...]
    quarter = frames // 4
    for h in range(1, quarter + 1):
        count = (h * delay) & (frames - 1)
        shifted = (count + (frames - quarter)) & (frames - 1)
        out_ref[2 * h - 2] = turn_value(count, frames).astype(jnp.bfloat16)
        out_ref[2 * h - 1] = turn_value(shifted, frames).astype(jnp.bfloat16)
    out_ref[2 * quarter] = jnp.where((delay & 1) == 1, -1.0, 1.0).astype(jnp.bfloat16)


def factor_stage(delay, frames):
    nfreq, trials = delay.shape
    rows = 32
    terms = frames // 2 + 1
    return pl.pallas_call(
        functools.partial(factor_kernel, frames),
        name="factors",
        grid=(nfreq // rows,),
        in_specs=[pl.BlockSpec((rows, trials), lambda i: (i, 0))],
        out_specs=pl.BlockSpec((terms, rows, trials), lambda i: (0, i, 0)),
        out_shape=jax.ShapeDtypeStruct((terms, nfreq, trials), jnp.bfloat16),
        compiler_params=params(),
        cost_estimate=cost(10 * terms * nfreq * trials, 2 * terms * nfreq * trials),
    )(delay)


def rounded(value):
    return float(np.asarray(value, np.float32).astype(jnp.bfloat16).astype(np.float32))


def turns(count, frames):
    angle = 2.0 * math.pi * (count % frames) / frames
    pair = []
    for value in (math.cos(angle), math.sin(angle)):
        pair.append(float(round(value)) if abs(value - round(value)) < 1e-12 else value)
    return pair


def weighted(terms):
    total = None
    for factor, value in terms:
        if factor == 0.0:
            continue
        term = value if factor == 1.0 else (-value if factor == -1.0 else factor * value)
        total = term if total is None else total + term
    return total


def harmonics_of(values, frames):
    half, quarter = frames // 2, frames // 4
    plus = [values[r] + values[r + half] for r in range(half)]
    minus = [values[r] - values[r + half] for r in range(half)]
    result = []
    for h in range(half + 1):
        base = minus if h % 2 else plus
        real, imag = [(1.0, base[0])], []
        for r in range(1, quarter):
            cosine, sine = (rounded(x) for x in turns(h * r, frames))
            other = base[half - r]
            even = base[r] - other if h % 2 else base[r] + other
            odd = base[r] + other if h % 2 else base[r] - other
            real.append((cosine, even))
            imag.append((-sine, odd))
        cosine, sine = (rounded(x) for x in turns(h * quarter, frames))
        real.append((cosine, base[quarter]))
        imag.append((-sine, base[quarter]))
        result.append((weighted(real), weighted(imag)))
    return result


def dedisperse_kernel(frames, nfreq, me_ref, *refs):
    arrived_refs, (factors_ref, out_ref, held, left, zero, slots, sems) = refs[:-7], refs[-7:]
    parts = len(arrived_refs)
    pairs, own, lanes = arrived_refs[0].shape
    half, quarter = frames // 2, frames // 4
    step, steps = pl.program_id(0), pl.num_programs(0)
    tile = slots.shape[3]

    def fetch(at, slot):
        cut = pl.ds(pl.multiple_of(at * tile, tile), tile)
        return pltpu.make_async_copy(factors_ref.at[:, :, cut], slots.at[slot], sems.at[slot])

    @pl.when(step == 0)
    def _():
        fetch(0, 0).start()
        low = lax.broadcasted_iota(jnp.int32, (own, lanes), 1) < lanes // 2
        zero[...] = jnp.zeros_like(zero)
        for d in range(parts):
            held[lax.rem(me_ref[0] + (parts - d), parts)] = arrived_refs[d][...]

        def one(j, carry):
            values = []
            for i in range(pairs):
                even = held[2 * j, i].astype(jnp.float32)
                odd = held[2 * j + 1, i].astype(jnp.float32)
                values.append(jnp.where(low, even, pltpu.roll(odd, lanes // 2, 1)))
                values.append(jnp.where(low, pltpu.roll(even, lanes // 2, 1), odd))
            terms = harmonics_of(values, frames)
            zero[...] += terms[0][0].astype(jnp.bfloat16).astype(jnp.float32)
            for h in range(1, half + 1):
                left[j, h - 1, :own, :] = terms[h][0].astype(jnp.bfloat16)
                if h < half:
                    left[j, h - 1, own:, :] = terms[h][1].astype(jnp.bfloat16)
            return carry

        lax.fori_loop(0, parts // 2, one, 0)

    slot = lax.rem(step, 2)

    @pl.when(step + 1 < steps)
    def _():
        fetch(step + 1, 1 - slot).start()

    fetch(step, slot).wait()
    factor_ref = slots.at[slot]
    scale = 1.0 / (frames * math.sqrt(nfreq))
    first = scale * jnp.sum(zero[...], axis=1, keepdims=True)
    real, imag = [], []
    parity = factor_ref[2 * quarter]
    for h in range(1, half):
        block = jnp.concatenate([left[j, h - 1] for j in range(parts // 2)], axis=1)
        base = min(h, half - h)
        cosines, sines = factor_ref[2 * base - 2], factor_ref[2 * base - 1]
        if h > quarter:
            cosines, sines = cosines * parity, sines * -parity
        by_cos = jnp.dot(block, cosines, preferred_element_type=jnp.float32)
        by_sin = jnp.dot(block, sines, preferred_element_type=jnp.float32)
        real.append((2.0 * scale) * (by_cos[:own] - by_sin[own:]))
        imag.append((2.0 * scale) * (by_sin[:own] + by_cos[own:]))
    block = jnp.concatenate([left[j, half - 1, :own, :] for j in range(parts // 2)], axis=1)
    last = scale * jnp.dot(block, parity, preferred_element_type=jnp.float32)
    for t in range(half):
        sums = []
        for odd in range(2):
            terms = []
            for h in range(2 - odd, half, 2):
                cosine, sine = turns(h * t, frames)
                terms.append((cosine, real[h - 1]))
                terms.append((-sine, imag[h - 1]))
            sums.append(weighted(terms))
        even = sums[0] + first + (last if t % 2 == 0 else -last)
        out_ref[:, t, :] = even + sums[1]
        out_ref[:, t + half, :] = even - sums[1]


def dedisperse_stage(me, arrived, factors, frames):
    pairs, own, lanes = arrived[0].shape
    parts = len(arrived)
    terms, nfreq, trials = factors.shape
    tile = 2 * LANES
    whole = lambda shape: pl.BlockSpec(shape, lambda i, me_ref: (0,) * len(shape))
    return pl.pallas_call(
        functools.partial(dedisperse_kernel, frames, nfreq),
        name="dedisperse",
        grid_spec=pltpu.PrefetchScalarGridSpec(
            num_scalar_prefetch=1,
            grid=(trials // tile,),
            in_specs=[whole(piece.shape) for piece in arrived]
            + [pl.BlockSpec(memory_space=pl.ANY)],
            out_specs=pl.BlockSpec((own, frames, tile), lambda i, me_ref: (0, 0, i)),
            scratch_shapes=[
                pltpu.VMEM((parts, pairs, own, lanes), jnp.bfloat16),
                pltpu.VMEM((parts // 2, frames // 2, 2 * own, lanes), jnp.bfloat16),
                pltpu.VMEM((own, lanes), jnp.float32),
                pltpu.VMEM((2, terms, nfreq, tile), jnp.bfloat16),
                pltpu.SemaphoreType.DMA((2,)),
            ],
        ),
        out_shape=jax.ShapeDtypeStruct((own, frames, trials), jnp.float32),
        compiler_params=params(),
        cost_estimate=cost(
            8 * own * terms * nfreq * trials, 2 * factors.size + 4 * own * frames * trials
        ),
    )(me, *arrived, factors)


def chunks_of(frames):
    end = max(2, frames // 4)
    return ((0, end, False), (end, frames - 2 * end, True), (frames - end, end, False))


def shifted(piece, by, parts):
    return lax.ppermute(piece, "wide", [(i, (i + by) % parts) for i in range(parts)])


def exchange(message, parts):
    if not isinstance(message, (list, tuple)):
        return [lax.all_to_all(message, "wide", split_axis=0, concat_axis=0, tiled=True)]
    return [message[0]] + [shifted(message[d], d, parts) for d in range(1, parts)]


def tiled_body(parts, raw, cell_feed, dm_delay):
    _, frames, _ = raw.shape
    me = lax.axis_index("wide").astype(jnp.int32)
    own = me.reshape(1)
    cuts = chunks_of(frames)
    messages = []
    for first, count, split in cuts:
        message = channelise(raw, own, first, count, parts, split)
        raw, cell_feed, dm_delay, message = lax.optimization_barrier(
            (raw, cell_feed, dm_delay, message)
        )
        messages.append(message)
    weights = beam_table(cell_feed, me, parts)
    factors = factor_stage(jnp.transpose(dm_delay), frames)
    messages[-1], factors = lax.optimization_barrier((messages[-1], factors))
    powers = []
    for message in messages[:-1]:
        power = beam_stage(weights, own, exchange(message, parts), frames, parts)
        weights, power = lax.optimization_barrier((weights, power))
        powers.append(power)
    tail = exchange(messages[-1], parts)
    early = beam_stage(weights, own, tail, frames, parts, powers, (0, 2))
    half = len(early)
    arrived = [early[0]] + [shifted(early[d], d, parts) for d in range(1, half)]
    weights, arrived[0] = lax.optimization_barrier((weights, arrived[0]))
    late = beam_stage(weights, own, tail, frames, parts, powers, (1, 2))
    arrived += [shifted(late[d], half + d, parts) for d in range(half)]
    return dedisperse_stage(own, arrived, factors, frames)


def fits(parts, raw_shape, cells, delay_shape):
    feed_dev, frames, samples = raw_shape
    trials, nfreq = delay_shape
    return (
        samples // parts == LANES
        and nfreq * 2 == samples
        and samples % (2 * LANES) == 0
        and feed_dev % 32 == 0
        and frames % 16 == 0
        and frames & (frames - 1) == 0
        and cells % 512 == 0
        and cells // parts == LANES // 2
        and trials % (2 * LANES) == 0
        and parts % 4 == 0
    )


def solution(mesh):
    parts = mesh.shape["wide"]

    def body(raw, cell_feed, dm_delay):
        if fits(parts, raw.shape, cell_feed.shape[0], dm_delay.shape):
            return tiled_body(parts, raw, cell_feed, dm_delay)
        return plain_body(raw, cell_feed, dm_delay)

    placed = (P(("grp", "wide"), None, None), P(), P())
    return jax.shard_map(
        body, mesh=mesh, in_specs=placed, out_specs=P(("grp", "wide"), None, None), check_vma=False
    )
```

profile of v0, /device:TPU:1, one launch (start us, length us, event | category | flops | bytes accessed | tf_op | source)
XLA Modules:
  0.0 332.1 jit_solution(1538251103119629998)
XLA Ops:
  0.0 12.7 %channelise.3 = bf16[16,4,2,64,128]{4,3,2,1,0:T(8,128)(2,1)} custom-call(s32[1]{0:T(128)} %bitcast.me_ref, f32[2,16,32,128]{3,2,1,0:T(8,128)} %constant.141.clone.coarse_ref, f32[2,16,64,128]{3,2,1,0:T(8,128)} %constant.142.clone.fine_ref, bf16[128,16,2048]{2,1,0:T(8,128)(2,1)} %raw_ref.3), custom_call_target="tpu_custom_call" | custom-call | flops 4294967296 | bytes 16777216 | tf_op jit(solution)/shard_map/channelise/pallas_call | solution.py:236
  12.7 7.3 %all-to-all-start = ((bf16[16,4,2,64,128]{4,3,2,1,0:T(8,128)(2,1)}), bf16[16,4,2,64,128]{4,3,2,1,0:T(8,128)(2,1)S(1)}, u32[]{:S(2)}, u32[]{:S(2)}) async-start(bf16[16,4,2,64,128]{4,3,2,1,0:T(8,128)(2,1)} %channelise.3), calls=%async_computation | async-start | bytes 4194304 | tf_op jit(solution)/shard_map/all_to_all | solution.py:587
  20.0 18.9 %channelise.4 = (bf16[8,2,64,128]{3,2,1,0:T(8,128)(2,1)}, bf16[8,2,64,128]{3,2,1,0:T(8,128)(2,1)}, bf16[8,2,64,128]{3,2,1,0:T(8,128)(2,1)}, bf16[8,2,64,128]{3,2...) custom-call(s32[1]{0:T(128)} %bitcast.me_ref, ...), custom_call_target="tpu_custom_call" | custom-call | flops 8589934592 | bytes 16777216 | tf_op jit(solution)/shard_map/channelise/pallas_call | solution.py:236
  38.9 1.7 collective-permute-start
  40.6 1.2 collective-permute-start.1
  41.7 0.4 collective-permute-start.2
  42.1 1.2 collective-permute-start.3
  43.3 2.2 collective-permute-start.4
  45.6 12.7 %channelise.5 = bf16[16,4,2,64,128]{4,3,2,1,0:T(8,128)(2,1)} custom-call(s32[1]{0:T(128)} %bitcast.me_ref, f32[2,16,32,128]{3,2,1,0:T(8,128)} %constant.141.clone.coarse_ref, f32[2,16,64,128]{3,2,1,0:T(8,128)} %constant.142.clone.fine_ref, bf16[128,16,2048]{2,1,0:T(8,128)(2,1)} %raw_ref.3), custom_call_target="tpu_custom_call" | custom-call | flops 4294967296 | bytes 16777216 | tf_op jit(solution)/shard_map/channelise/pallas_call | solution.py:236
  58.3 5.3 %copy.14 = s32[1024,1024]{0,1:T(8,128)} copy(s32[1024,1024]{1,0:T(8,128)} %param.11) | data formatting | bytes 8388608 | tf_op jit(solution)/shard_map/optimization_barrier | solution.py:599
  63.6 29.4 %factors.1.refs_16_ = bf16[9,1024,1024]{2,1,0:T(8,128)(2,1)} custom-call(s32[1024,1024]{1,0:T(8,128)} %bitcast.11), custom_call_target="tpu_custom_call" | custom-call | flops 94371840 | bytes 18874368 | tf_op jit(solution)/shard_map/factors/pallas_call | solution.py:414
  93.1 1.3 copy-done.1
  94.4 5.0 %all-to-all-start.1 = ((bf16[16,4,2,64,128]{4,3,2,1,0:T(8,128)(2,1)}), bf16[16,4,2,64,128]{4,3,2,1,0:T(8,128)(2,1)S(1)}, u32[]{:S(2)}, u32[]{:S(2)}) async-start(bf16[16,4,2,64,128]{4,3,2,1,0:T(8,128)(2,1)} %channelise.5), calls=%async_computation.1 | async-start | bytes 4194304 | tf_op jit(solution)/shard_map/all_to_all | solution.py:587
  99.4 1.6 select_reduce_fusion
  101.2 4.5 %multiply_convert_fusion = (bf16[256,1024]{1,0:T(8,128)(2,1)S(1)}, bf16[256,1024]{1,0:T(8,128)(2,1)S(1)}) fusion(s32[1024]{0:T(1024)S(1)} %get-tuple-element.146), kind=kLoop, calls=%fused_computation.19 | loop fusion | flops 4718592 | bytes 1052672 | tf_op jit(solution)/shard_map/convert_element_type | solution.py:272
  105.7 0.1 neg.29
  105.8 0.1 neg.31
  105.9 0.2 broadcast_in_dim.79
  106.2 0.3 broadcast_in_dim.81
  106.4 0.3 broadcast_in_dim.77
  106.7 2.6 negate_select_fusion.3
  109.3 0.1 broadcast_in_dim.68
  109.3 0.1 broadcast_in_dim.69
  109.4 4.6 %pad_maximum_fusion = bf16[2,16,64,1024]{3,2,1,0:T(8,128)(2,1)} fusion(bf16[1,16,64,1024]{3,2,1,0:T(8,128)(2,1)} %get-tuple-element.142, bf16[1,16,64,1024]{3,2,1,0:T(8,128)(2,1)} %get-tuple-element.141), kind=kLoop, calls=%fused_computation.8 | loop fusion | flops 2097152 | bytes 8388608 | tf_op jit(solution)/shard_map/stack | solution.py:278
  114.1 5.0 %gather_fusion = bf16[16,2,64,1024]{3,2,1,0:T(8,128)(2,1)} fusion(bf16[2,16,64,1024]{3,2,1,0:T(8,128)(2,1)} %pad_maximum_fusion, s32[1024]{0:T(1024)S(1)} %pad_clamp_fusion), kind=kCustom, calls=%fused_computation | custom fusion | bytes 8388672 | tf_op jit(solution)/shard_map/jit(_take)/gather | solution.py:280
  119.1 2.8 copy.13
  121.9 2.3 collective-permute-start.5
  124.3 2.7 collective-permute-start.6
  127.0 0.3 collective-permute-start.7
  127.3 3.0 collective-permute-start.8
  130.3 1.2 collective-permute-start.9
  131.6 2.7 bitcast_select_fusion.weight_ref
  134.3 39.4 %collective-permute-done.5.refs_6_ = bf16[8,2,64,128]{3,2,1,0:T(8,128)(2,1)S(1)} collective-permute-done((bf16[8,2,64,128]{3,2,1,0:T(8,128)(2,1)S(1)}, bf16[8,2,64,128]{3,2,1,0:T(8,128)(2,1)S(1)}, u32[]{:S(2)}, u32[]{:S(2)}) %collective-permute-start.5) | collective-permute-done | bytes 262176 | tf_op jit(solution)/shard_map/ppermute | solution.py:582
  173.8 16.6 %collective-permute-start.10 = (bf16[8,2,64,128]{3,2,1,0:T(8,128)(2,1)S(1)}, bf16[8,2,64,128]{3,2,1,0:T(8,128)(2,1)S(1)}, u32[]{:S(2)}, u32[]{:S(2)}) collective-permute-start(bf16[8,2,64,128]{3,2,1,0:T(8,128)(2,1)S(1)} %copy-done.25), channel_id=1, source_target_pairs={{0,11},{1,12},{2,13},{3,14},{4,15},{5,0},{6,1},{7,2},{8,3},{9,4},{... | collective-permute-start | bytes 786440 | tf_op jit(solution)/shard_map/ppermute | solution.py:582
  190.3 8.1 %collective-permute-start.11 = (bf16[8,2,64,128]{3,2,1,0:T(8,128)(2,1)S(1)}, bf16[8,2,64,128]{3,2,1,0:T(8,128)(2,1)S(1)}, u32[]{:S(2)}, u32[]{:S(2)}) collective-permute-start(bf16[8,2,64,128]{3,2,1,0:T(8,128)(2,1)S(1)} %copy-done.23), channel_id=1, source_target_pairs={{0,12},{1,13},{2,14},{3,15},{4,0},{5,1},{6,2},{7,3},{8,4},{9,5},{1... | collective-permute-start | bytes 786440 | tf_op jit(solution)/shard_map/ppermute | solution.py:582
  198.5 8.1 %collective-permute-start.12 = (bf16[8,2,64,128]{3,2,1,0:T(8,128)(2,1)S(1)}, bf16[8,2,64,128]{3,2,1,0:T(8,128)(2,1)S(1)}, u32[]{:S(2)}, u32[]{:S(2)}) collective-permute-start(bf16[8,2,64,128]{3,2,1,0:T(8,128)(2,1)S(1)} %copy-done.21), channel_id=1, source_target_pairs={{0,13},{1,14},{2,15},{3,0},{4,1},{5,2},{6,3},{7,4},{8,5},{9,6},{10... | collective-permute-start | bytes 786440 | tf_op jit(solution)/shard_map/ppermute | solution.py:582
  206.6 2.5 collective-permute-start.13
  209.2 0.7 copy-done.36
  209.9 10.5 %beams.4.refs_1_ = f32[2,1024,128]{2,1,0:T(8,128)} custom-call(s32[1]{0:T(128)} %bitcast.me_ref, bf16[2,1024,1024]{2,1,0:T(8,128)(2,1)} %bitcast_select_fusion.weight_ref, bf16[16,4,2,64,128]{4,3,2,1,0:T(8,128)(2,1)} %copy-done.1), custom_call_target="tpu_custom_call" | custom-call | flops 4294967296 | bytes 10485760 | tf_op jit(solution)/shard_map/beams/pallas_call | solution.py:368
  220.4 0.6 copy-done.37
  221.1 0.1 copy-done.38
  221.2 0.1 copy-done.40
  221.3 0.7 copy-done.41
  222.1 18.9 %beams.5.refs_2_ = f32[4,1024,128]{2,1,0:T(8,128)} custom-call(s32[1]{0:T(128)} %bitcast.me_ref, bf16[2,1024,1024]{2,1,0:T(8,128)(2,1)} %bitcast_select_fusion.weight_ref, bf16[8,2,64,128]{3,2,1,0:T(8,128)(2,1)} %get-tuple-element.100.refs_0_, bf16[8,2,64,128]{3,2,1,0:T(8,128)(2,1)} %copy-done.18, bf16[8,2,64,128]{3,2,1,0:T(8,128)(2,1)} %copy-done.20, ...), custom_call_target="tpu_custom_call" | custom-call | flops 8589934592 | bytes 12582912 | tf_op jit(solution)/shard_map/beams/pallas_call | solution.py:368
  241.0 1.3 copy-done
  242.3 6.8 %beams.6 = (bf16[8,64,128]{2,1,0:T(8,128)(2,1)}, bf16[8,64,128]{2,1,0:T(8,128)(2,1)}, bf16[8,64,128]{2,1,0:T(8,128)(2,1)}, bf16[8,64,128]{2,1,0:T(8,128)(2,1)}, ...) custom-call(s32[1]{0:T(128)} %bitcast.me_ref, ...), custom_call_target="tpu_custom_call" | custom-call | flops 2147483648 | bytes 10485760 | tf_op jit(solution)/shard_map/beams/pallas_call | solution.py:368
  249.2 7.0 %beams.7 = (bf16[8,64,128]{2,1,0:T(8,128)(2,1)}, bf16[8,64,128]{2,1,0:T(8,128)(2,1)}, bf16[8,64,128]{2,1,0:T(8,128)(2,1)}, bf16[8,64,128]{2,1,0:T(8,128)(2,1)}, ...) custom-call(s32[1]{0:T(128)} %bitcast.me_ref, ...), custom_call_target="tpu_custom_call" | custom-call | flops 2147483648 | bytes 10485760 | tf_op jit(solution)/shard_map/beams/pallas_call | solution.py:368
  256.1 2.1 collective-permute-start.22
  258.2 2.0 collective-permute-start.23
  260.2 0.3 collective-permute-start.24
  260.5 4.3 %collective-permute-start.25 = (bf16[8,64,128]{2,1,0:T(8,128)(2,1)}, bf16[8,64,128]{2,1,0:T(8,128)(2,1)S(1)}, u32[]{:S(2)}, u32[]{:S(2)}) collective-permute-start(bf16[8,64,128]{2,1,0:T(8,128)(2,1)} %get-tuple-element.135), channel_id=1, source_target_pairs={{0,11},{1,12},{2,13},{3,14},{4,15},{5,0},{6,1},{7,2},{8,3},{9,4},{... | collective-permute-start | bytes 393224 | tf_op jit(solution)/shard_map/ppermute | solution.py:582
  264.8 14.0 %collective-permute-start.27 = (bf16[8,64,128]{2,1,0:T(8,128)(2,1)}, bf16[8,64,128]{2,1,0:T(8,128)(2,1)S(1)}, u32[]{:S(2)}, u32[]{:S(2)}) collective-permute-start(bf16[8,64,128]{2,1,0:T(8,128)(2,1)} %get-tuple-element.137), channel_id=1, source_target_pairs={{0,13},{1,14},{2,15},{3,0},{4,1},{5,2},{6,3},{7,4},{8,5},{9,6},{10... | collective-permute-start | bytes 393224 | tf_op jit(solution)/shard_map/ppermute | solution.py:582
  278.8 1.3 collective-permute-start.28
  280.1 2.7 collective-permute-start.29
  282.9 6.2 %collective-permute-start.16 = (bf16[8,64,128]{2,1,0:T(8,128)(2,1)S(1)}, bf16[8,64,128]{2,1,0:T(8,128)(2,1)S(1)}, u32[]{:S(2)}, u32[]{:S(2)}) collective-permute-start(bf16[8,64,128]{2,1,0:T(8,128)(2,1)S(1)} %copy-done.47), channel_id=1, source_target_pairs={{0,2},{1,3},{2,4},{3,5},{4,6},{5,7},{6,8},{7,9},{8,10},{9,11},{10,... | collective-permute-start | bytes 393224 | tf_op jit(solution)/shard_map/ppermute | solution.py:582
  289.3 5.5 %collective-permute-start.19 = (bf16[8,64,128]{2,1,0:T(8,128)(2,1)S(1)}, bf16[8,64,128]{2,1,0:T(8,128)(2,1)S(1)}, u32[]{:S(2)}, u32[]{:S(2)}) collective-permute-start(bf16[8,64,128]{2,1,0:T(8,128)(2,1)S(1)} %copy-done.44), channel_id=1, source_target_pairs={{0,5},{1,6},{2,7},{3,8},{4,9},{5,10},{6,11},{7,12},{8,13},{9,14},{... | collective-permute-start | bytes 393224 | tf_op jit(solution)/shard_map/ppermute | solution.py:582
  294.9 3.4 %collective-permute-done.16.refs_2_ = bf16[8,64,128]{2,1,0:T(8,128)(2,1)S(1)} collective-permute-done((bf16[8,64,128]{2,1,0:T(8,128)(2,1)S(1)}, bf16[8,64,128]{2,1,0:T(8,128)(2,1)S(1)}, u32[]{:S(2)}, u32[]{:S(2)}) %collective-permute-start.16) | collective-permute-done | bytes 131104 | tf_op jit(solution)/shard_map/ppermute | solution.py:582
  298.3 1.3 collective-permute-done.17.refs_3_
  299.6 0.6 collective-permute-done.19.refs_5_
  300.2 16.8 %collective-permute-done.20.refs_6_ = bf16[8,64,128]{2,1,0:T(8,128)(2,1)S(1)} collective-permute-done((bf16[8,64,128]{2,1,0:T(8,128)(2,1)S(1)}, bf16[8,64,128]{2,1,0:T(8,128)(2,1)S(1)}, u32[]{:S(2)}, u32[]{:S(2)}) %collective-permute-start.20) | collective-permute-done | bytes 131104 | tf_op jit(solution)/shard_map/ppermute | solution.py:582
  317.0 0.2 collective-permute-done.21.refs_7_
  317.3 0.3 copy-done.15
  317.6 0.6 copy-done.16
  318.3 13.6 %dedisperse.1 = f32[64,16,1024]{2,1,0:T(8,128)} custom-call(s32[1]{0:T(128)} %bitcast.me_ref, bf16[8,64,128]{2,1,0:T(8,128)(2,1)} %get-tuple-element.123.refs_0_, bf16[8,64,128]{2,1,0:T(8,128)(2,1)} %copy-done.10, bf16[8,64,128]{2,1,0:T(8,128)(2,1)} %copy-done.11, bf16[8,64,128]{2,1,0:T(8,128)(2,1)} %copy-done.12, bf16[8,64,128]{2,1,0:T(8,128)(2,1)} %copy-done.13, ...), custom_call_target="tpu_custom_call" | custom-call | flops 4831838208 | bytes 23068672 | tf_op jit(solution)/shard_map/dedisperse/pallas_call | solution.py:551
  (136 shorter events, 0.7 us)
Async XLA Ops:
  12.7 80.4 %all-to-all-start = ((bf16[16,4,2,64,128]{4,3,2,1,0:T(8,128)(2,1)}), bf16[16,4,2,64,128]{4,3,2,1,0:T(8,128)(2,1)S(1)}, u32[]{:S(2)}, u32[]{:S(2)}) async-start(bf16[16,4,2,64,128]{4,3,2,1,0:T(8,128)(2,1)} %channelise.3), calls=%async_computation | async-start | bytes 4194304 | tf_op jit(solution)/shard_map/all_to_all | solution.py:587
  38.9 83.0 %collective-permute-start = (bf16[8,2,64,128]{3,2,1,0:T(8,128)(2,1)}, bf16[8,2,64,128]{3,2,1,0:T(8,128)(2,1)S(1)}, u32[]{:S(2)}, u32[]{:S(2)}) collective-permute-start(bf16[8,2,64,128]{3,2,1,0:T(8,128)(2,1)} %get-tuple-element.101), channel_id=1, source_target_pairs={{0,1},{1,2},{2,3},{3,4},{4,5},{5,6},{6,7},{7,8},{8,9},{9,10},{10,1... | collective-permute-start | bytes 786440 | tf_op jit(solution)/shard_map/ppermute | solution.py:582
  40.6 83.7 %collective-permute-start.1 = (bf16[8,2,64,128]{3,2,1,0:T(8,128)(2,1)}, bf16[8,2,64,128]{3,2,1,0:T(8,128)(2,1)S(1)}, u32[]{:S(2)}, u32[]{:S(2)}) collective-permute-start(bf16[8,2,64,128]{3,2,1,0:T(8,128)(2,1)} %get-tuple-element.102), channel_id=1, source_target_pairs={{0,2},{1,3},{2,4},{3,5},{4,6},{5,7},{6,8},{7,9},{8,10},{9,11},{10,... | collective-permute-start | bytes 786440 | tf_op jit(solution)/shard_map/ppermute | solution.py:582
  41.7 85.2 %collective-permute-start.2 = (bf16[8,2,64,128]{3,2,1,0:T(8,128)(2,1)}, bf16[8,2,64,128]{3,2,1,0:T(8,128)(2,1)S(1)}, u32[]{:S(2)}, u32[]{:S(2)}) collective-permute-start(bf16[8,2,64,128]{3,2,1,0:T(8,128)(2,1)} %get-tuple-element.103), channel_id=1, source_target_pairs={{0,3},{1,4},{2,5},{3,6},{4,7},{5,8},{6,9},{7,10},{8,11},{9,12},{10... | collective-permute-start | bytes 786440 | tf_op jit(solution)/shard_map/ppermute | solution.py:582
  42.1 85.2 %collective-permute-start.3 = (bf16[8,2,64,128]{3,2,1,0:T(8,128)(2,1)}, bf16[8,2,64,128]{3,2,1,0:T(8,128)(2,1)S(1)}, u32[]{:S(2)}, u32[]{:S(2)}) collective-permute-start(bf16[8,2,64,128]{3,2,1,0:T(8,128)(2,1)} %get-tuple-element.104), channel_id=1, source_target_pairs={{0,4},{1,5},{2,6},{3,7},{4,8},{5,9},{6,10},{7,11},{8,12},{9,13},{1... | collective-permute-start | bytes 786440 | tf_op jit(solution)/shard_map/ppermute | solution.py:582
  43.3 87.0 %collective-permute-start.4 = (bf16[8,2,64,128]{3,2,1,0:T(8,128)(2,1)}, bf16[8,2,64,128]{3,2,1,0:T(8,128)(2,1)S(1)}, u32[]{:S(2)}, u32[]{:S(2)}) collective-permute-start(bf16[8,2,64,128]{3,2,1,0:T(8,128)(2,1)} %get-tuple-element.105), channel_id=1, source_target_pairs={{0,5},{1,6},{2,7},{3,8},{4,9},{5,10},{6,11},{7,12},{8,13},{9,14},{... | collective-permute-start | bytes 786440 | tf_op jit(solution)/shard_map/ppermute | solution.py:582
  94.4 146.6 %all-to-all-start.1 = ((bf16[16,4,2,64,128]{4,3,2,1,0:T(8,128)(2,1)}), bf16[16,4,2,64,128]{4,3,2,1,0:T(8,128)(2,1)S(1)}, u32[]{:S(2)}, u32[]{:S(2)}) async-start(bf16[16,4,2,64,128]{4,3,2,1,0:T(8,128)(2,1)} %channelise.5), calls=%async_computation.1 | async-start | bytes 4194304 | tf_op jit(solution)/shard_map/all_to_all | solution.py:587
  119.0 8.3 %copy-start.28 = (bf16[8,2,64,128]{3,2,1,0:T(8,128)(2,1)S(1)}, bf16[8,2,64,128]{3,2,1,0:T(8,128)(2,1)}, u32[]{:S(2)}) copy-start(bf16[8,2,64,128]{3,2,1,0:T(8,128)(2,1)} %get-tuple-element.109) | copy-start | bytes 786436
  119.0 11.3 %copy-start.27 = (bf16[8,2,64,128]{3,2,1,0:T(8,128)(2,1)S(1)}, bf16[8,2,64,128]{3,2,1,0:T(8,128)(2,1)}, u32[]{:S(2)}) copy-start(bf16[8,2,64,128]{3,2,1,0:T(8,128)(2,1)} %get-tuple-element.110) | copy-start | bytes 786436
  121.9 51.9 %copy-start.25 = (bf16[8,2,64,128]{3,2,1,0:T(8,128)(2,1)S(1)}, bf16[8,2,64,128]{3,2,1,0:T(8,128)(2,1)}, u32[]{:S(2)}) copy-start(bf16[8,2,64,128]{3,2,1,0:T(8,128)(2,1)} %get-tuple-element.111) | copy-start | bytes 786436
  121.9 68.4 %copy-start.23 = (bf16[8,2,64,128]{3,2,1,0:T(8,128)(2,1)S(1)}, bf16[8,2,64,128]{3,2,1,0:T(8,128)(2,1)}, u32[]{:S(2)}) copy-start(bf16[8,2,64,128]{3,2,1,0:T(8,128)(2,1)} %get-tuple-element.112) | copy-start | bytes 786436
  121.9 76.6 %copy-start.21 = (bf16[8,2,64,128]{3,2,1,0:T(8,128)(2,1)S(1)}, bf16[8,2,64,128]{3,2,1,0:T(8,128)(2,1)}, u32[]{:S(2)}) copy-start(bf16[8,2,64,128]{3,2,1,0:T(8,128)(2,1)} %get-tuple-element.113) | copy-start | bytes 786436
  121.9 84.7 %copy-start.19 = (bf16[8,2,64,128]{3,2,1,0:T(8,128)(2,1)S(1)}, bf16[8,2,64,128]{3,2,1,0:T(8,128)(2,1)}, u32[]{:S(2)}) copy-start(bf16[8,2,64,128]{3,2,1,0:T(8,128)(2,1)} %get-tuple-element.114) | copy-start | bytes 786436
  121.9 88.0 %copy-start.17 = (bf16[8,2,64,128]{3,2,1,0:T(8,128)(2,1)S(1)}, bf16[8,2,64,128]{3,2,1,0:T(8,128)(2,1)}, u32[]{:S(2)}) copy-start(bf16[8,2,64,128]{3,2,1,0:T(8,128)(2,1)} %get-tuple-element.115) | copy-start | bytes 786436
  121.9 12.4 %copy-start.18 = (bf16[8,2,64,128]{3,2,1,0:T(8,128)(2,1)}, bf16[8,2,64,128]{3,2,1,0:T(8,128)(2,1)S(1)}, u32[]{:S(2)}) copy-start(bf16[8,2,64,128]{3,2,1,0:T(8,128)(2,1)S(1)} %collective-permute-done.refs_1_) | copy-start | bytes 786436
  121.9 51.8 %collective-permute-start.5 = (bf16[8,2,64,128]{3,2,1,0:T(8,128)(2,1)S(1)}, bf16[8,2,64,128]{3,2,1,0:T(8,128)(2,1)S(1)}, u32[]{:S(2)}, u32[]{:S(2)}) collective-permute-start(bf16[8,2,64,128]{3,2,1,0:T(8,128)(2,1)S(1)} %copy-done.31), channel_id=1, source_target_pairs={{0,6},{1,7},{2,8},{3,9},{4,10},{5,11},{6,12},{7,13},{8,14},{9,15},... | collective-permute-start | bytes 786440 | tf_op jit(solution)/shard_map/ppermute | solution.py:582
  124.3 10.1 %copy-start.20 = (bf16[8,2,64,128]{3,2,1,0:T(8,128)(2,1)}, bf16[8,2,64,128]{3,2,1,0:T(8,128)(2,1)S(1)}, u32[]{:S(2)}) copy-start(bf16[8,2,64,128]{3,2,1,0:T(8,128)(2,1)S(1)} %collective-permute-done.1.refs_2_) | copy-start | bytes 786436
  124.3 66.1 %collective-permute-start.6 = (bf16[8,2,64,128]{3,2,1,0:T(8,128)(2,1)S(1)}, bf16[8,2,64,128]{3,2,1,0:T(8,128)(2,1)S(1)}, u32[]{:S(2)}, u32[]{:S(2)}) collective-permute-start(bf16[8,2,64,128]{3,2,1,0:T(8,128)(2,1)S(1)} %copy-done.30), channel_id=1, source_target_pairs={{0,7},{1,8},{2,9},{3,10},{4,11},{5,12},{6,13},{7,14},{8,15},{9,0},... | collective-permute-start | bytes 786440 | tf_op jit(solution)/shard_map/ppermute | solution.py:582
  127.0 71.5 %collective-permute-start.7 = (bf16[8,2,64,128]{3,2,1,0:T(8,128)(2,1)S(1)}, bf16[8,2,64,128]{3,2,1,0:T(8,128)(2,1)S(1)}, u32[]{:S(2)}, u32[]{:S(2)}) collective-permute-start(bf16[8,2,64,128]{3,2,1,0:T(8,128)(2,1)S(1)} %copy-done.29), channel_id=1, source_target_pairs={{0,8},{1,9},{2,10},{3,11},{4,12},{5,13},{6,14},{7,15},{8,0},{9,1},... | collective-permute-start | bytes 786440 | tf_op jit(solution)/shard_map/ppermute | solution.py:582
  127.3 79.3 %collective-permute-start.8 = (bf16[8,2,64,128]{3,2,1,0:T(8,128)(2,1)S(1)}, bf16[8,2,64,128]{3,2,1,0:T(8,128)(2,1)S(1)}, u32[]{:S(2)}, u32[]{:S(2)}) collective-permute-start(bf16[8,2,64,128]{3,2,1,0:T(8,128)(2,1)S(1)} %copy-done.28), channel_id=1, source_target_pairs={{0,9},{1,10},{2,11},{3,12},{4,13},{5,14},{6,15},{7,0},{8,1},{9,2},... | collective-permute-start | bytes 786440 | tf_op jit(solution)/shard_map/ppermute | solution.py:582
  130.3 78.8 %collective-permute-start.9 = (bf16[8,2,64,128]{3,2,1,0:T(8,128)(2,1)S(1)}, bf16[8,2,64,128]{3,2,1,0:T(8,128)(2,1)S(1)}, u32[]{:S(2)}, u32[]{:S(2)}) collective-permute-start(bf16[8,2,64,128]{3,2,1,0:T(8,128)(2,1)S(1)} %copy-done.27), channel_id=1, source_target_pairs={{0,10},{1,11},{2,12},{3,13},{4,14},{5,15},{6,0},{7,1},{8,2},{9,3},... | collective-permute-start | bytes 786440 | tf_op jit(solution)/shard_map/ppermute | solution.py:582
  173.8 35.4 %copy-start.32 = (bf16[8,2,64,128]{3,2,1,0:T(8,128)(2,1)}, bf16[8,2,64,128]{3,2,1,0:T(8,128)(2,1)S(1)}, u32[]{:S(2)}) copy-start(bf16[8,2,64,128]{3,2,1,0:T(8,128)(2,1)S(1)} %collective-permute-done.5.refs_6_) | copy-start | bytes 786436
  173.8 46.6 %collective-permute-start.10 = (bf16[8,2,64,128]{3,2,1,0:T(8,128)(2,1)S(1)}, bf16[8,2,64,128]{3,2,1,0:T(8,128)(2,1)S(1)}, u32[]{:S(2)}, u32[]{:S(2)}) collective-permute-start(bf16[8,2,64,128]{3,2,1,0:T(8,128)(2,1)S(1)} %copy-done.25), channel_id=1, source_target_pairs={{0,11},{1,12},{2,13},{3,14},{4,15},{5,0},{6,1},{7,2},{8,3},{9,4},{... | collective-permute-start | bytes 786440 | tf_op jit(solution)/shard_map/ppermute | solution.py:582
  190.3 18.8 %copy-start.33 = (bf16[8,2,64,128]{3,2,1,0:T(8,128)(2,1)}, bf16[8,2,64,128]{3,2,1,0:T(8,128)(2,1)S(1)}, u32[]{:S(2)}) copy-start(bf16[8,2,64,128]{3,2,1,0:T(8,128)(2,1)S(1)} %collective-permute-done.6.refs_7_) | copy-start | bytes 786436
  190.3 30.0 %collective-permute-start.11 = (bf16[8,2,64,128]{3,2,1,0:T(8,128)(2,1)S(1)}, bf16[8,2,64,128]{3,2,1,0:T(8,128)(2,1)S(1)}, u32[]{:S(2)}, u32[]{:S(2)}) collective-permute-start(bf16[8,2,64,128]{3,2,1,0:T(8,128)(2,1)S(1)} %copy-done.23), channel_id=1, source_target_pairs={{0,12},{1,13},{2,14},{3,15},{4,0},{5,1},{6,2},{7,3},{8,4},{9,5},{1... | collective-permute-start | bytes 786440 | tf_op jit(solution)/shard_map/ppermute | solution.py:582
  198.5 10.7 %copy-start.34 = (bf16[8,2,64,128]{3,2,1,0:T(8,128)(2,1)}, bf16[8,2,64,128]{3,2,1,0:T(8,128)(2,1)S(1)}, u32[]{:S(2)}) copy-start(bf16[8,2,64,128]{3,2,1,0:T(8,128)(2,1)S(1)} %collective-permute-done.7.refs_8_) | copy-start | bytes 786436
  198.5 21.9 %collective-permute-start.12 = (bf16[8,2,64,128]{3,2,1,0:T(8,128)(2,1)S(1)}, bf16[8,2,64,128]{3,2,1,0:T(8,128)(2,1)S(1)}, u32[]{:S(2)}, u32[]{:S(2)}) collective-permute-start(bf16[8,2,64,128]{3,2,1,0:T(8,128)(2,1)S(1)} %copy-done.21), channel_id=1, source_target_pairs={{0,13},{1,14},{2,15},{3,0},{4,1},{5,2},{6,3},{7,4},{8,5},{9,6},{10... | collective-permute-start | bytes 786440 | tf_op jit(solution)/shard_map/ppermute | solution.py:582
  206.6 13.8 %collective-permute-start.13 = (bf16[8,2,64,128]{3,2,1,0:T(8,128)(2,1)S(1)}, bf16[8,2,64,128]{3,2,1,0:T(8,128)(2,1)S(1)}, u32[]{:S(2)}, u32[]{:S(2)}) collective-permute-start(bf16[8,2,64,128]{3,2,1,0:T(8,128)(2,1)S(1)} %copy-done.19), channel_id=1, source_target_pairs={{0,14},{1,15},{2,0},{3,1},{4,2},{5,3},{6,4},{7,5},{8,6},{9,7},{10,... | collective-permute-start | bytes 786440 | tf_op jit(solution)/shard_map/ppermute | solution.py:582
  209.9 10.6 %collective-permute-start.14 = (bf16[8,2,64,128]{3,2,1,0:T(8,128)(2,1)S(1)}, bf16[8,2,64,128]{3,2,1,0:T(8,128)(2,1)S(1)}, u32[]{:S(2)}, u32[]{:S(2)}) collective-permute-start(bf16[8,2,64,128]{3,2,1,0:T(8,128)(2,1)S(1)} %copy-done.17), channel_id=1, source_target_pairs={{0,15},{1,0},{2,1},{3,2},{4,3},{5,4},{6,5},{7,6},{8,7},{9,8},{10,9... | collective-permute-start | bytes 786440 | tf_op jit(solution)/shard_map/ppermute | solution.py:582
  249.1 33.8 %copy-start.48 = (bf16[8,64,128]{2,1,0:T(8,128)(2,1)S(1)}, bf16[8,64,128]{2,1,0:T(8,128)(2,1)}, u32[]{:S(2)}) copy-start(bf16[8,64,128]{2,1,0:T(8,128)(2,1)} %get-tuple-element.124) | copy-start | bytes 393220
  249.1 33.8 %copy-start.47 = (bf16[8,64,128]{2,1,0:T(8,128)(2,1)S(1)}, bf16[8,64,128]{2,1,0:T(8,128)(2,1)}, u32[]{:S(2)}) copy-start(bf16[8,64,128]{2,1,0:T(8,128)(2,1)} %get-tuple-element.125) | copy-start | bytes 393220
  249.1 40.0 %copy-start.46 = (bf16[8,64,128]{2,1,0:T(8,128)(2,1)S(1)}, bf16[8,64,128]{2,1,0:T(8,128)(2,1)}, u32[]{:S(2)}) copy-start(bf16[8,64,128]{2,1,0:T(8,128)(2,1)} %get-tuple-element.126) | copy-start | bytes 393220
  249.1 40.1 %copy-start.45 = (bf16[8,64,128]{2,1,0:T(8,128)(2,1)S(1)}, bf16[8,64,128]{2,1,0:T(8,128)(2,1)}, u32[]{:S(2)}) copy-start(bf16[8,64,128]{2,1,0:T(8,128)(2,1)} %get-tuple-element.127) | copy-start | bytes 393220
  249.1 40.2 %copy-start.44 = (bf16[8,64,128]{2,1,0:T(8,128)(2,1)S(1)}, bf16[8,64,128]{2,1,0:T(8,128)(2,1)}, u32[]{:S(2)}) copy-start(bf16[8,64,128]{2,1,0:T(8,128)(2,1)} %get-tuple-element.128) | copy-start | bytes 393220
  249.1 45.7 %copy-start.43 = (bf16[8,64,128]{2,1,0:T(8,128)(2,1)S(1)}, bf16[8,64,128]{2,1,0:T(8,128)(2,1)}, u32[]{:S(2)}) copy-start(bf16[8,64,128]{2,1,0:T(8,128)(2,1)} %get-tuple-element.129) | copy-start | bytes 393220
  249.1 49.1 %copy-start.42 = (bf16[8,64,128]{2,1,0:T(8,128)(2,1)S(1)}, bf16[8,64,128]{2,1,0:T(8,128)(2,1)}, u32[]{:S(2)}) copy-start(bf16[8,64,128]{2,1,0:T(8,128)(2,1)} %get-tuple-element.130) | copy-start | bytes 393220
  256.1 8.7 %collective-permute-start.22 = (bf16[8,64,128]{2,1,0:T(8,128)(2,1)}, bf16[8,64,128]{2,1,0:T(8,128)(2,1)S(1)}, u32[]{:S(2)}, u32[]{:S(2)}) collective-permute-start(bf16[8,64,128]{2,1,0:T(8,128)(2,1)} %get-tuple-element.132), channel_id=1, source_target_pairs={{0,8},{1,9},{2,10},{3,11},{4,12},{5,13},{6,14},{7,15},{8,0},{9,1},... | collective-permute-start | bytes 393224 | tf_op jit(solution)/shard_map/ppermute | solution.py:582
  258.2 20.6 %collective-permute-start.23 = (bf16[8,64,128]{2,1,0:T(8,128)(2,1)}, bf16[8,64,128]{2,1,0:T(8,128)(2,1)S(1)}, u32[]{:S(2)}, u32[]{:S(2)}) collective-permute-start(bf16[8,64,128]{2,1,0:T(8,128)(2,1)} %get-tuple-element.133), channel_id=1, source_target_pairs={{0,9},{1,10},{2,11},{3,12},{4,13},{5,14},{6,15},{7,0},{8,1},{9,2},... | collective-permute-start | bytes 393224 | tf_op jit(solution)/shard_map/ppermute | solution.py:582
  260.2 19.9 %collective-permute-start.24 = (bf16[8,64,128]{2,1,0:T(8,128)(2,1)}, bf16[8,64,128]{2,1,0:T(8,128)(2,1)S(1)}, u32[]{:S(2)}, u32[]{:S(2)}) collective-permute-start(bf16[8,64,128]{2,1,0:T(8,128)(2,1)} %get-tuple-element.134), channel_id=1, source_target_pairs={{0,10},{1,11},{2,12},{3,13},{4,14},{5,15},{6,0},{7,1},{8,2},{9,3},... | collective-permute-start | bytes 393224 | tf_op jit(solution)/shard_map/ppermute | solution.py:582
  260.5 22.3 %collective-permute-start.25 = (bf16[8,64,128]{2,1,0:T(8,128)(2,1)}, bf16[8,64,128]{2,1,0:T(8,128)(2,1)S(1)}, u32[]{:S(2)}, u32[]{:S(2)}) collective-permute-start(bf16[8,64,128]{2,1,0:T(8,128)(2,1)} %get-tuple-element.135), channel_id=1, source_target_pairs={{0,11},{1,12},{2,13},{3,14},{4,15},{5,0},{6,1},{7,2},{8,3},{9,4},{... | collective-permute-start | bytes 393224 | tf_op jit(solution)/shard_map/ppermute | solution.py:582
  264.8 18.1 %collective-permute-start.26 = (bf16[8,64,128]{2,1,0:T(8,128)(2,1)}, bf16[8,64,128]{2,1,0:T(8,128)(2,1)S(1)}, u32[]{:S(2)}, u32[]{:S(2)}) collective-permute-start(bf16[8,64,128]{2,1,0:T(8,128)(2,1)} %get-tuple-element.136), channel_id=1, source_target_pairs={{0,12},{1,13},{2,14},{3,15},{4,0},{5,1},{6,2},{7,3},{8,4},{9,5},{1... | collective-permute-start | bytes 393224 | tf_op jit(solution)/shard_map/ppermute | solution.py:582
  264.8 52.4 %copy-start.2 = (bf16[8,64,128]{2,1,0:T(8,128)(2,1)}, bf16[8,64,128]{2,1,0:T(8,128)(2,1)S(1)}, u32[]{:S(2)}) copy-start(bf16[8,64,128]{2,1,0:T(8,128)(2,1)S(1)} %collective-permute-done.22.refs_8_) | copy-start | bytes 393220
  264.8 24.3 %collective-permute-start.27 = (bf16[8,64,128]{2,1,0:T(8,128)(2,1)}, bf16[8,64,128]{2,1,0:T(8,128)(2,1)S(1)}, u32[]{:S(2)}, u32[]{:S(2)}) collective-permute-start(bf16[8,64,128]{2,1,0:T(8,128)(2,1)} %get-tuple-element.137), channel_id=1, source_target_pairs={{0,13},{1,14},{2,15},{3,0},{4,1},{5,2},{6,3},{7,4},{8,5},{9,6},{10... | collective-permute-start | bytes 393224 | tf_op jit(solution)/shard_map/ppermute | solution.py:582
  278.8 38.4 %copy-start.3 = (bf16[8,64,128]{2,1,0:T(8,128)(2,1)}, bf16[8,64,128]{2,1,0:T(8,128)(2,1)S(1)}, u32[]{:S(2)}) copy-start(bf16[8,64,128]{2,1,0:T(8,128)(2,1)S(1)} %collective-permute-done.23.refs_9_) | copy-start | bytes 393220
  278.8 10.3 %collective-permute-start.28 = (bf16[8,64,128]{2,1,0:T(8,128)(2,1)}, bf16[8,64,128]{2,1,0:T(8,128)(2,1)S(1)}, u32[]{:S(2)}, u32[]{:S(2)}) collective-permute-start(bf16[8,64,128]{2,1,0:T(8,128)(2,1)} %get-tuple-element.138), channel_id=1, source_target_pairs={{0,14},{1,15},{2,0},{3,1},{4,2},{5,3},{6,4},{7,5},{8,6},{9,7},{10,... | collective-permute-start | bytes 393224 | tf_op jit(solution)/shard_map/ppermute | solution.py:582
  280.1 37.1 %copy-start.4 = (bf16[8,64,128]{2,1,0:T(8,128)(2,1)}, bf16[8,64,128]{2,1,0:T(8,128)(2,1)S(1)}, u32[]{:S(2)}) copy-start(bf16[8,64,128]{2,1,0:T(8,128)(2,1)S(1)} %collective-permute-done.24.refs_10_) | copy-start | bytes 393220
  280.1 9.2 %collective-permute-start.29 = (bf16[8,64,128]{2,1,0:T(8,128)(2,1)}, bf16[8,64,128]{2,1,0:T(8,128)(2,1)S(1)}, u32[]{:S(2)}, u32[]{:S(2)}) collective-permute-start(bf16[8,64,128]{2,1,0:T(8,128)(2,1)} %get-tuple-element.139), channel_id=1, source_target_pairs={{0,15},{1,0},{2,1},{3,2},{4,3},{5,4},{6,5},{7,6},{8,7},{9,8},{10,9... | collective-permute-start | bytes 393224 | tf_op jit(solution)/shard_map/ppermute | solution.py:582
  282.9 34.4 %copy-start.5 = (bf16[8,64,128]{2,1,0:T(8,128)(2,1)}, bf16[8,64,128]{2,1,0:T(8,128)(2,1)S(1)}, u32[]{:S(2)}) copy-start(bf16[8,64,128]{2,1,0:T(8,128)(2,1)S(1)} %collective-permute-done.25.refs_11_) | copy-start | bytes 393220
  282.9 12.0 %collective-permute-start.15 = (bf16[8,64,128]{2,1,0:T(8,128)(2,1)S(1)}, bf16[8,64,128]{2,1,0:T(8,128)(2,1)S(1)}, u32[]{:S(2)}, u32[]{:S(2)}) collective-permute-start(bf16[8,64,128]{2,1,0:T(8,128)(2,1)S(1)} %copy-done.48), channel_id=1, source_target_pairs={{0,1},{1,2},{2,3},{3,4},{4,5},{5,6},{6,7},{7,8},{8,9},{9,10},{10,1... | collective-permute-start | bytes 393224 | tf_op jit(solution)/shard_map/ppermute | solution.py:582
  282.9 34.3 %copy-start.6 = (bf16[8,64,128]{2,1,0:T(8,128)(2,1)}, bf16[8,64,128]{2,1,0:T(8,128)(2,1)S(1)}, u32[]{:S(2)}) copy-start(bf16[8,64,128]{2,1,0:T(8,128)(2,1)S(1)} %collective-permute-done.26.refs_12_) | copy-start | bytes 393220
  282.9 15.3 %collective-permute-start.16 = (bf16[8,64,128]{2,1,0:T(8,128)(2,1)S(1)}, bf16[8,64,128]{2,1,0:T(8,128)(2,1)S(1)}, u32[]{:S(2)}, u32[]{:S(2)}) collective-permute-start(bf16[8,64,128]{2,1,0:T(8,128)(2,1)S(1)} %copy-done.47), channel_id=1, source_target_pairs={{0,2},{1,3},{2,4},{3,5},{4,6},{5,7},{6,8},{7,9},{8,10},{9,11},{10,... | collective-permute-start | bytes 393224 | tf_op jit(solution)/shard_map/ppermute | solution.py:582
  289.1 28.1 %copy-start.7 = (bf16[8,64,128]{2,1,0:T(8,128)(2,1)}, bf16[8,64,128]{2,1,0:T(8,128)(2,1)S(1)}, u32[]{:S(2)}) copy-start(bf16[8,64,128]{2,1,0:T(8,128)(2,1)S(1)} %collective-permute-done.27.refs_13_) | copy-start | bytes 393220
  289.1 10.5 %collective-permute-start.17 = (bf16[8,64,128]{2,1,0:T(8,128)(2,1)S(1)}, bf16[8,64,128]{2,1,0:T(8,128)(2,1)S(1)}, u32[]{:S(2)}, u32[]{:S(2)}) collective-permute-start(bf16[8,64,128]{2,1,0:T(8,128)(2,1)S(1)} %copy-done.46), channel_id=1, source_target_pairs={{0,3},{1,4},{2,5},{3,6},{4,7},{5,8},{6,9},{7,10},{8,11},{9,12},{10... | collective-permute-start | bytes 393224 | tf_op jit(solution)/shard_map/ppermute | solution.py:582
  289.2 28.0 %copy-start.8 = (bf16[8,64,128]{2,1,0:T(8,128)(2,1)}, bf16[8,64,128]{2,1,0:T(8,128)(2,1)S(1)}, u32[]{:S(2)}) copy-start(bf16[8,64,128]{2,1,0:T(8,128)(2,1)S(1)} %collective-permute-done.28.refs_14_) | copy-start | bytes 393220
  289.2 10.4 %collective-permute-start.18 = (bf16[8,64,128]{2,1,0:T(8,128)(2,1)S(1)}, bf16[8,64,128]{2,1,0:T(8,128)(2,1)S(1)}, u32[]{:S(2)}, u32[]{:S(2)}) collective-permute-start(bf16[8,64,128]{2,1,0:T(8,128)(2,1)S(1)} %copy-done.45), channel_id=1, source_target_pairs={{0,4},{1,5},{2,6},{3,7},{4,8},{5,9},{6,10},{7,11},{8,12},{9,13},{1... | collective-permute-start | bytes 393224 | tf_op jit(solution)/shard_map/ppermute | solution.py:582
  289.3 28.0 %copy-start.9 = (bf16[8,64,128]{2,1,0:T(8,128)(2,1)}, bf16[8,64,128]{2,1,0:T(8,128)(2,1)S(1)}, u32[]{:S(2)}) copy-start(bf16[8,64,128]{2,1,0:T(8,128)(2,1)S(1)} %collective-permute-done.29.refs_15_) | copy-start | bytes 393220
  289.3 10.9 %collective-permute-start.19 = (bf16[8,64,128]{2,1,0:T(8,128)(2,1)S(1)}, bf16[8,64,128]{2,1,0:T(8,128)(2,1)S(1)}, u32[]{:S(2)}, u32[]{:S(2)}) collective-permute-start(bf16[8,64,128]{2,1,0:T(8,128)(2,1)S(1)} %copy-done.44), channel_id=1, source_target_pairs={{0,5},{1,6},{2,7},{3,8},{4,9},{5,10},{6,11},{7,12},{8,13},{9,14},{... | collective-permute-start | bytes 393224 | tf_op jit(solution)/shard_map/ppermute | solution.py:582
  294.8 22.4 %copy-start.10 = (bf16[8,64,128]{2,1,0:T(8,128)(2,1)}, bf16[8,64,128]{2,1,0:T(8,128)(2,1)S(1)}, u32[]{:S(2)}) copy-start(bf16[8,64,128]{2,1,0:T(8,128)(2,1)S(1)} %collective-permute-done.15.refs_1_) | copy-start | bytes 393220
  294.8 22.2 %collective-permute-start.20 = (bf16[8,64,128]{2,1,0:T(8,128)(2,1)S(1)}, bf16[8,64,128]{2,1,0:T(8,128)(2,1)S(1)}, u32[]{:S(2)}, u32[]{:S(2)}) collective-permute-start(bf16[8,64,128]{2,1,0:T(8,128)(2,1)S(1)} %copy-done.43), channel_id=1, source_target_pairs={{0,6},{1,7},{2,8},{3,9},{4,10},{5,11},{6,12},{7,13},{8,14},{9,15},... | collective-permute-start | bytes 393224 | tf_op jit(solution)/shard_map/ppermute | solution.py:582
  298.3 19.0 %copy-start.11 = (bf16[8,64,128]{2,1,0:T(8,128)(2,1)}, bf16[8,64,128]{2,1,0:T(8,128)(2,1)S(1)}, u32[]{:S(2)}) copy-start(bf16[8,64,128]{2,1,0:T(8,128)(2,1)S(1)} %collective-permute-done.16.refs_2_) | copy-start | bytes 393220
  298.3 18.9 %collective-permute-start.21 = (bf16[8,64,128]{2,1,0:T(8,128)(2,1)S(1)}, bf16[8,64,128]{2,1,0:T(8,128)(2,1)S(1)}, u32[]{:S(2)}, u32[]{:S(2)}) collective-permute-start(bf16[8,64,128]{2,1,0:T(8,128)(2,1)S(1)} %copy-done.42), channel_id=1, source_target_pairs={{0,7},{1,8},{2,9},{3,10},{4,11},{5,12},{6,13},{7,14},{8,15},{9,0},... | collective-permute-start | bytes 393224 | tf_op jit(solution)/shard_map/ppermute | solution.py:582
  299.6 17.7 %copy-start.12 = (bf16[8,64,128]{2,1,0:T(8,128)(2,1)}, bf16[8,64,128]{2,1,0:T(8,128)(2,1)S(1)}, u32[]{:S(2)}) copy-start(bf16[8,64,128]{2,1,0:T(8,128)(2,1)S(1)} %collective-permute-done.17.refs_3_) | copy-start | bytes 393220
  299.6 17.7 %copy-start.13 = (bf16[8,64,128]{2,1,0:T(8,128)(2,1)}, bf16[8,64,128]{2,1,0:T(8,128)(2,1)S(1)}, u32[]{:S(2)}) copy-start(bf16[8,64,128]{2,1,0:T(8,128)(2,1)S(1)} %collective-permute-done.18.refs_4_) | copy-start | bytes 393220
  300.2 17.1 %copy-start.14 = (bf16[8,64,128]{2,1,0:T(8,128)(2,1)}, bf16[8,64,128]{2,1,0:T(8,128)(2,1)S(1)}, u32[]{:S(2)}) copy-start(bf16[8,64,128]{2,1,0:T(8,128)(2,1)S(1)} %collective-permute-done.19.refs_5_) | copy-start | bytes 393220
  (18 other events, 51.8 us)
where the time goes:
time: 333 us; the launch traced here: 332 us
  Pallas kernels  130 us (39%)
  starting transfers between devices  103 us (31%)
  waiting for transfers between devices  61.8 us (19%)
  local copies, waits for them, and re-layouts  20.2 us (6%)
  other arithmetic  16.3 us (5%)
    ppermute x30, starting transfers between devices, shifted(): lax.ppermute(piece, 'wide', [(i, (i + by) % parts) for i in range(parts)])  90.2 us
    ppermute x30, waiting for transfers between devices, shifted(): lax.ppermute(piece, 'wide', [(i, (i + by) % parts) for i in range(parts)])  61.8 us
    pallas_call x3, Pallas kernels, channelise(): pl.pallas_call(functools.partial(channelise_kernel, low, first, frames),...  44.3 us
    pallas_call x4, Pallas kernels, beam_stage(): pl.pallas_call(functools.partial(beam_kernel, frames, len(arrived), len(b...  43.1 us
    pallas_call x1, Pallas kernels, factor_stage(): pl.pallas_call(functools.partial(factor_kernel, frames), name='factors',...  29.4 us
    pallas_call x1, Pallas kernels, dedisperse_stage(): pl.pallas_call(functools.partial(dedisperse_kernel, frames, nfreq), name=...  13.6 us
    all_to_all x2, starting transfers between devices, exchange(): lax.all_to_all(message, 'wide', split_axis=0, concat_axis=0, tiled=True)  12.3 us
    gather x2, local copies, waits for them, and re-layouts, beam_table(): jnp.take(table.reshape(2, parts, own, beams), order, axis=1)  7.78 us
  transfers between devices with their start and end apart: 32, of which 6 were waited for; matrix products, arithmetic and copies ran while one was open for 9% of the time, Pallas kernels for 27%

commit v1 on v0

--- a/solution.py
+++ b/solution.py
@@ -276,7 +276,7 @@
     real = jnp.where(odd, -sine, cosine)
     imag = jnp.where(odd, -cosine, -sine)
     table = jnp.stack([jnp.where(minus, -real, real), jnp.where(minus, -imag, imag)])
-    order = (me + jnp.arange(parts, dtype=jnp.int32)) % parts
+    order = (me + parts // 4 + jnp.arange(parts, dtype=jnp.int32)) % parts
     return jnp.take(table.reshape(2, parts, own, beams), order, axis=1).reshape(2, beams, beams)
 
 
@@ -610,11 +610,15 @@
         powers.append(power)
     tail = exchange(messages[-1], parts)
     early = beam_stage(weights, own, tail, frames, parts, powers, (0, 2))
-    half = len(early)
-    arrived = [early[0]] + [shifted(early[d], d, parts) for d in range(1, half)]
-    weights, arrived[0] = lax.optimization_barrier((weights, arrived[0]))
+    half, turn = len(early), parts // 4
+    arrived = [None] * parts
+    for i, piece in enumerate(early):
+        arrived[turn + i] = shifted(piece, turn + i, parts)
+    weights, powers[0] = lax.optimization_barrier((weights, powers[0]))
     late = beam_stage(weights, own, tail, frames, parts, powers, (1, 2))
-    arrived += [shifted(late[d], half + d, parts) for d in range(half)]
+    for i, piece in enumerate(late):
+        by = (turn + half + i) % parts
+        arrived[by] = shifted(piece, by, parts) if by else piece
     return dedisperse_stage(own, arrived, factors, frames)
 
 

time: 333 us -> 322 us (0.967)
  the two profiles are of different devices: /device:TPU:1 before, /device:TPU:13 now
where the time goes in v1:
time: 322 us; the launch traced here: 321 us
  Pallas kernels  130 us (40%)
  waiting for transfers between devices  99.9 us (31%)
  starting transfers between devices  53.8 us (17%)
  local copies, waits for them, and re-layouts  19.7 us (6%)
  other arithmetic  16.4 us (5%)
    ppermute x30, waiting for transfers between devices, shifted(): lax.ppermute(piece, 'wide', [(i, (i + by) % parts) for i in range(parts)])  99.8 us
    pallas_call x3, Pallas kernels, channelise(): pl.pallas_call(functools.partial(channelise_kernel, low, first, frames),...  44.3 us
    pallas_call x4, Pallas kernels, beam_stage(): pl.pallas_call(functools.partial(beam_kernel, frames, len(arrived), len(b...  43 us
    ppermute x30, starting transfers between devices, shifted(): lax.ppermute(piece, 'wide', [(i, (i + by) % parts) for i in range(parts)])  42.5 us
    pallas_call x1, Pallas kernels, factor_stage(): pl.pallas_call(functools.partial(factor_kernel, frames), name='factors',...  29.4 us
    pallas_call x1, Pallas kernels, dedisperse_stage(): pl.pallas_call(functools.partial(dedisperse_kernel, frames, nfreq), name=...  13.6 us
    all_to_all x2, starting transfers between devices, exchange(): lax.all_to_all(message, 'wide', split_axis=0, concat_axis=0, tiled=True)  11.3 us
    gather x2, local copies, waits for them, and re-layouts, beam_table(): jnp.take(table.reshape(2, parts, own, beams), order, axis=1)  7.8 us
  transfers between devices with their start and end apart: 32, of which 13 were waited for; matrix products, arithmetic and copies ran while one was open for 10% of the time, Pallas kernels for 30%

profile of v1, /device:TPU:13, one launch (start us, length us, event | category | flops | bytes accessed | tf_op | source)
XLA Modules:
  0.0 320.6 jit_solution(2300532097973824397)
XLA Ops:
  0.0 12.7 %channelise.3 = bf16[16,4,2,64,128]{4,3,2,1,0:T(8,128)(2,1)} custom-call(s32[1]{0:T(128)} %bitcast.me_ref, f32[2,16,32,128]{3,2,1,0:T(8,128)} %constant.141.clone.coarse_ref, f32[2,16,64,128]{3,2,1,0:T(8,128)} %constant.142.clone.fine_ref, bf16[128,16,2048]{2,1,0:T(8,128)(2,1)} %raw_ref.3), custom_call_target="tpu_custom_call" | custom-call | flops 4294967296 | bytes 16777216 | tf_op jit(solution)/shard_map/channelise/pallas_call | solution.py:236
  12.7 6.5 %all-to-all-start = ((bf16[16,4,2,64,128]{4,3,2,1,0:T(8,128)(2,1)}), bf16[16,4,2,64,128]{4,3,2,1,0:T(8,128)(2,1)S(1)}, u32[]{:S(2)}, u32[]{:S(2)}) async-start(bf16[16,4,2,64,128]{4,3,2,1,0:T(8,128)(2,1)} %channelise.3), calls=%async_computation | async-start | bytes 4194304 | tf_op jit(solution)/shard_map/all_to_all | solution.py:587
  19.2 18.9 %channelise.4 = (bf16[8,2,64,128]{3,2,1,0:T(8,128)(2,1)}, bf16[8,2,64,128]{3,2,1,0:T(8,128)(2,1)}, bf16[8,2,64,128]{3,2,1,0:T(8,128)(2,1)}, bf16[8,2,64,128]{3,2...) custom-call(s32[1]{0:T(128)} %bitcast.me_ref, ...), custom_call_target="tpu_custom_call" | custom-call | flops 8589934592 | bytes 16777216 | tf_op jit(solution)/shard_map/channelise/pallas_call | solution.py:236
  38.1 1.5 collective-permute-start
  39.6 1.2 collective-permute-start.1
  40.8 0.4 collective-permute-start.2
  41.2 0.8 collective-permute-start.3
  41.9 2.9 collective-permute-start.4
  44.9 12.7 %channelise.5 = bf16[16,4,2,64,128]{4,3,2,1,0:T(8,128)(2,1)} custom-call(s32[1]{0:T(128)} %bitcast.me_ref, f32[2,16,32,128]{3,2,1,0:T(8,128)} %constant.141.clone.coarse_ref, f32[2,16,64,128]{3,2,1,0:T(8,128)} %constant.142.clone.fine_ref, bf16[128,16,2048]{2,1,0:T(8,128)(2,1)} %raw_ref.3), custom_call_target="tpu_custom_call" | custom-call | flops 4294967296 | bytes 16777216 | tf_op jit(solution)/shard_map/channelise/pallas_call | solution.py:236
  57.6 5.3 %copy.14 = s32[1024,1024]{0,1:T(8,128)} copy(s32[1024,1024]{1,0:T(8,128)} %param.11) | data formatting | bytes 8388608 | tf_op jit(solution)/shard_map/optimization_barrier | solution.py:599
  62.9 29.4 %factors.1.refs_16_ = bf16[9,1024,1024]{2,1,0:T(8,128)(2,1)} custom-call(s32[1024,1024]{1,0:T(8,128)} %bitcast.11), custom_call_target="tpu_custom_call" | custom-call | flops 94371840 | bytes 18874368 | tf_op jit(solution)/shard_map/factors/pallas_call | solution.py:414
  92.4 0.1 all-to-all-done.refs_0_
  92.5 1.3 copy-done.1
  93.8 4.8 %all-to-all-start.1 = ((bf16[16,4,2,64,128]{4,3,2,1,0:T(8,128)(2,1)}), bf16[16,4,2,64,128]{4,3,2,1,0:T(8,128)(2,1)S(1)}, u32[]{:S(2)}, u32[]{:S(2)}) async-start(bf16[16,4,2,64,128]{4,3,2,1,0:T(8,128)(2,1)} %channelise.5), calls=%async_computation.1 | async-start | bytes 4194304 | tf_op jit(solution)/shard_map/all_to_all | solution.py:587
  98.5 1.6 select_reduce_fusion
  100.3 4.5 %multiply_convert_fusion = (bf16[256,1024]{1,0:T(8,128)(2,1)S(1)}, bf16[256,1024]{1,0:T(8,128)(2,1)S(1)}) fusion(s32[1024]{0:T(1024)S(1)} %get-tuple-element.146), kind=kLoop, calls=%fused_computation.19 | loop fusion | flops 4718592 | bytes 1052672 | tf_op jit(solution)/shard_map/convert_element_type | solution.py:272
  104.8 0.1 neg.29
  104.9 0.1 neg.31
  105.1 0.2 broadcast_in_dim.79
  105.3 0.3 broadcast_in_dim.81
  105.6 0.3 broadcast_in_dim.77
  105.8 2.6 negate_select_fusion.3
  108.6 4.6 %pad_maximum_fusion = bf16[2,16,64,1024]{3,2,1,0:T(8,128)(2,1)} fusion(bf16[1,16,64,1024]{3,2,1,0:T(8,128)(2,1)} %get-tuple-element.142, bf16[1,16,64,1024]{3,2,1,0:T(8,128)(2,1)} %get-tuple-element.141), kind=kLoop, calls=%fused_computation.8 | loop fusion | flops 2097152 | bytes 8388608 | tf_op jit(solution)/shard_map/stack | solution.py:278
  113.2 5.0 %gather_fusion = bf16[16,2,64,1024]{3,2,1,0:T(8,128)(2,1)} fusion(bf16[2,16,64,1024]{3,2,1,0:T(8,128)(2,1)} %pad_maximum_fusion, s32[1024]{0:T(1024)S(1)} %pad_clamp_fusion), kind=kCustom, calls=%fused_computation | custom fusion | bytes 8388672 | tf_op jit(solution)/shard_map/jit(_take)/gather | solution.py:280
  118.2 2.8 copy.13
  121.1 2.1 collective-permute-start.5
  123.3 0.9 collective-permute-start.6
  124.2 2.1 collective-permute-start.7
  126.3 0.4 collective-permute-start.8
  126.7 3.0 collective-permute-start.9
  129.7 2.7 bitcast_select_fusion.weight_ref
  132.4 50.5 %collective-permute-done.5.refs_6_ = bf16[8,2,64,128]{3,2,1,0:T(8,128)(2,1)S(1)} collective-permute-done((bf16[8,2,64,128]{3,2,1,0:T(8,128)(2,1)S(1)}, bf16[8,2,64,128]{3,2,1,0:T(8,128)(2,1)S(1)}, u32[]{:S(2)}, u32[]{:S(2)}) %collective-permute-start.5) | collective-permute-done | bytes 262176 | tf_op jit(solution)/shard_map/ppermute | solution.py:582
  183.0 5.6 %collective-permute-done.6.refs_7_ = bf16[8,2,64,128]{3,2,1,0:T(8,128)(2,1)S(1)} collective-permute-done((bf16[8,2,64,128]{3,2,1,0:T(8,128)(2,1)S(1)}, bf16[8,2,64,128]{3,2,1,0:T(8,128)(2,1)S(1)}, u32[]{:S(2)}, u32[]{:S(2)}) %collective-permute-start.6) | collective-permute-done | bytes 262176 | tf_op jit(solution)/shard_map/ppermute | solution.py:582
  188.6 11.2 %collective-permute-done.7.refs_8_ = bf16[8,2,64,128]{3,2,1,0:T(8,128)(2,1)S(1)} collective-permute-done((bf16[8,2,64,128]{3,2,1,0:T(8,128)(2,1)S(1)}, bf16[8,2,64,128]{3,2,1,0:T(8,128)(2,1)S(1)}, u32[]{:S(2)}, u32[]{:S(2)}) %collective-permute-start.7) | collective-permute-done | bytes 262176 | tf_op jit(solution)/shard_map/ppermute | solution.py:582
  199.9 0.6 copy-done.34
  200.5 0.1 copy-done.35
  200.6 0.7 copy-done.36
  201.3 3.7 %collective-permute-start.14 = (bf16[8,2,64,128]{3,2,1,0:T(8,128)(2,1)S(1)}, bf16[8,2,64,128]{3,2,1,0:T(8,128)(2,1)S(1)}, u32[]{:S(2)}, u32[]{:S(2)}) collective-permute-start(bf16[8,2,64,128]{3,2,1,0:T(8,128)(2,1)S(1)} %copy-done.17), channel_id=1, source_target_pairs={{0,15},{1,0},{2,1},{3,2},{4,3},{5,4},{6,5},{7,6},{8,7},{9,8},{10,9... | collective-permute-start | bytes 786440 | tf_op jit(solution)/shard_map/ppermute | solution.py:582
  205.0 10.4 %beams.4.refs_1_ = f32[2,1024,128]{2,1,0:T(8,128)} custom-call(s32[1]{0:T(128)} %bitcast.me_ref, bf16[2,1024,1024]{2,1,0:T(8,128)(2,1)} %bitcast_select_fusion.weight_ref, bf16[16,4,2,64,128]{4,3,2,1,0:T(8,128)(2,1)} %copy-done.1), custom_call_target="tpu_custom_call" | custom-call | flops 4294967296 | bytes 10485760 | tf_op jit(solution)/shard_map/beams/pallas_call | solution.py:368
  215.5 5.7 %collective-permute-done.13.refs_14_ = bf16[8,2,64,128]{3,2,1,0:T(8,128)(2,1)S(1)} collective-permute-done((bf16[8,2,64,128]{3,2,1,0:T(8,128)(2,1)S(1)}, bf16[8,2,64,128]{3,2,1,0:T(8,128)(2,1)S(1)}, u32[]{:S(2)}, u32[]{:S(2)}) %collective-permute-start.13) | collective-permute-done | bytes 262176 | tf_op jit(solution)/shard_map/ppermute | solution.py:582
  221.2 0.6 collective-permute-done.14.refs_15_
  221.8 0.1 copy-done.40
  221.9 0.7 copy-done.41
  222.6 18.9 %beams.5.refs_2_ = f32[4,1024,128]{2,1,0:T(8,128)} custom-call(s32[1]{0:T(128)} %bitcast.me_ref, bf16[2,1024,1024]{2,1,0:T(8,128)(2,1)} %bitcast_select_fusion.weight_ref, bf16[8,2,64,128]{3,2,1,0:T(8,128)(2,1)} %get-tuple-element.100.refs_0_, bf16[8,2,64,128]{3,2,1,0:T(8,128)(2,1)} %copy-done.18, bf16[8,2,64,128]{3,2,1,0:T(8,128)(2,1)} %copy-done.20, ...), custom_call_target="tpu_custom_call" | custom-call | flops 8589934592 | bytes 12582912 | tf_op jit(solution)/shard_map/beams/pallas_call | solution.py:368
  241.6 1.3 copy-done
  242.9 6.8 %beams.7 = (bf16[8,64,128]{2,1,0:T(8,128)(2,1)}, bf16[8,64,128]{2,1,0:T(8,128)(2,1)}, bf16[8,64,128]{2,1,0:T(8,128)(2,1)}, bf16[8,64,128]{2,1,0:T(8,128)(2,1)}, ...) custom-call(s32[1]{0:T(128)} %bitcast.me_ref, ...), custom_call_target="tpu_custom_call" | custom-call | flops 2147483648 | bytes 10485760 | tf_op jit(solution)/shard_map/beams/pallas_call | solution.py:368
  249.7 3.6 %collective-permute-start.19 = (bf16[8,64,128]{2,1,0:T(8,128)(2,1)}, bf16[8,64,128]{2,1,0:T(8,128)(2,1)S(1)}, u32[]{:S(2)}, u32[]{:S(2)}) collective-permute-start(bf16[8,64,128]{2,1,0:T(8,128)(2,1)} %get-tuple-element.129), channel_id=1, source_target_pairs={{0,5},{1,6},{2,7},{3,8},{4,9},{5,10},{6,11},{7,12},{8,13},{9,14},{... | collective-permute-start | bytes 393224 | tf_op jit(solution)/shard_map/ppermute | solution.py:582
  253.3 0.3 collective-permute-start.21
  253.5 2.4 collective-permute-start.22
  255.9 6.8 %beams.6 = (bf16[8,64,128]{2,1,0:T(8,128)(2,1)}, bf16[8,64,128]{2,1,0:T(8,128)(2,1)}, bf16[8,64,128]{2,1,0:T(8,128)(2,1)}, bf16[8,64,128]{2,1,0:T(8,128)(2,1)}, ...) custom-call(s32[1]{0:T(128)} %bitcast.me_ref, ...), custom_call_target="tpu_custom_call" | custom-call | flops 2147483648 | bytes 10485760 | tf_op jit(solution)/shard_map/beams/pallas_call | solution.py:368
  262.8 0.7 collective-permute-start.23
  263.4 8.8 %collective-permute-done.19.refs_5_ = bf16[8,64,128]{2,1,0:T(8,128)(2,1)S(1)} collective-permute-done((bf16[8,64,128]{2,1,0:T(8,128)(2,1)}, bf16[8,64,128]{2,1,0:T(8,128)(2,1)S(1)}, u32[]{:S(2)}, u32[]{:S(2)}) %collective-permute-start.19) | collective-permute-done | bytes 131104 | tf_op jit(solution)/shard_map/ppermute | solution.py:582
  272.3 2.8 collective-permute-done.20.refs_6_
  275.1 2.9 collective-permute-start.25
  278.0 5.6 %collective-permute-done.22.refs_8_ = bf16[8,64,128]{2,1,0:T(8,128)(2,1)S(1)} collective-permute-done((bf16[8,64,128]{2,1,0:T(8,128)(2,1)}, bf16[8,64,128]{2,1,0:T(8,128)(2,1)S(1)}, u32[]{:S(2)}, u32[]{:S(2)}) %collective-permute-start.22) | collective-permute-done | bytes 131104 | tf_op jit(solution)/shard_map/ppermute | solution.py:582
  283.6 3.1 collective-permute-start.26
  286.8 0.2 collective-permute-start.27
  286.9 8.1 %collective-permute-start.28 = (bf16[8,64,128]{2,1,0:T(8,128)(2,1)}, bf16[8,64,128]{2,1,0:T(8,128)(2,1)S(1)}, u32[]{:S(2)}, u32[]{:S(2)}) collective-permute-start(bf16[8,64,128]{2,1,0:T(8,128)(2,1)} %get-tuple-element.138), channel_id=1, source_target_pairs={{0,14},{1,15},{2,0},{3,1},{4,2},{5,3},{6,4},{7,5},{8,6},{9,7},{10,... | collective-permute-start | bytes 393224 | tf_op jit(solution)/shard_map/ppermute | solution.py:582
  295.0 2.3 collective-permute-start.29
  297.3 2.0 collective-permute-done.26.refs_12_
  299.3 6.2 %collective-permute-done.28.refs_14_ = bf16[8,64,128]{2,1,0:T(8,128)(2,1)S(1)} collective-permute-done((bf16[8,64,128]{2,1,0:T(8,128)(2,1)}, bf16[8,64,128]{2,1,0:T(8,128)(2,1)S(1)}, u32[]{:S(2)}, u32[]{:S(2)}) %collective-permute-start.28) | collective-permute-done | bytes 131104 | tf_op jit(solution)/shard_map/ppermute | solution.py:582
  305.5 0.6 collective-permute-done.29.refs_15_
  306.3 0.5 copy-done.16
  306.8 13.6 %dedisperse.1 = f32[64,16,1024]{2,1,0:T(8,128)} custom-call(s32[1]{0:T(128)} %bitcast.me_ref, bf16[8,64,128]{2,1,0:T(8,128)(2,1)} %get-tuple-element.124.refs_0_, bf16[8,64,128]{2,1,0:T(8,128)(2,1)} %copy-done.10, bf16[8,64,128]{2,1,0:T(8,128)(2,1)} %copy-done.11, bf16[8,64,128]{2,1,0:T(8,128)(2,1)} %copy-done.12, bf16[8,64,128]{2,1,0:T(8,128)(2,1)} %copy-done.2, ...), custom_call_target="tpu_custom_call" | custom-call | flops 4831838208 | bytes 23068672 | tf_op jit(solution)/shard_map/dedisperse/pallas_call | solution.py:551
  (128 shorter events, 0.8 us)
Async XLA Ops:
  12.7 79.8 %all-to-all-start = ((bf16[16,4,2,64,128]{4,3,2,1,0:T(8,128)(2,1)}), bf16[16,4,2,64,128]{4,3,2,1,0:T(8,128)(2,1)S(1)}, u32[]{:S(2)}, u32[]{:S(2)}) async-start(bf16[16,4,2,64,128]{4,3,2,1,0:T(8,128)(2,1)} %channelise.3), calls=%async_computation | async-start | bytes 4194304 | tf_op jit(solution)/shard_map/all_to_all | solution.py:587
  38.1 83.0 %collective-permute-start = (bf16[8,2,64,128]{3,2,1,0:T(8,128)(2,1)}, bf16[8,2,64,128]{3,2,1,0:T(8,128)(2,1)S(1)}, u32[]{:S(2)}, u32[]{:S(2)}) collective-permute-start(bf16[8,2,64,128]{3,2,1,0:T(8,128)(2,1)} %get-tuple-element.101), channel_id=1, source_target_pairs={{0,1},{1,2},{2,3},{3,4},{4,5},{5,6},{6,7},{7,8},{8,9},{9,10},{10,1... | collective-permute-start | bytes 786440 | tf_op jit(solution)/shard_map/ppermute | solution.py:582
  39.6 83.7 %collective-permute-start.1 = (bf16[8,2,64,128]{3,2,1,0:T(8,128)(2,1)}, bf16[8,2,64,128]{3,2,1,0:T(8,128)(2,1)S(1)}, u32[]{:S(2)}, u32[]{:S(2)}) collective-permute-start(bf16[8,2,64,128]{3,2,1,0:T(8,128)(2,1)} %get-tuple-element.102), channel_id=1, source_target_pairs={{0,2},{1,3},{2,4},{3,5},{4,6},{5,7},{6,8},{7,9},{8,10},{9,11},{10,... | collective-permute-start | bytes 786440 | tf_op jit(solution)/shard_map/ppermute | solution.py:582
  40.8 83.4 %collective-permute-start.2 = (bf16[8,2,64,128]{3,2,1,0:T(8,128)(2,1)}, bf16[8,2,64,128]{3,2,1,0:T(8,128)(2,1)S(1)}, u32[]{:S(2)}, u32[]{:S(2)}) collective-permute-start(bf16[8,2,64,128]{3,2,1,0:T(8,128)(2,1)} %get-tuple-element.103), channel_id=1, source_target_pairs={{0,3},{1,4},{2,5},{3,6},{4,7},{5,8},{6,9},{7,10},{8,11},{9,12},{10... | collective-permute-start | bytes 786440 | tf_op jit(solution)/shard_map/ppermute | solution.py:582
  41.2 85.2 %collective-permute-start.3 = (bf16[8,2,64,128]{3,2,1,0:T(8,128)(2,1)}, bf16[8,2,64,128]{3,2,1,0:T(8,128)(2,1)S(1)}, u32[]{:S(2)}, u32[]{:S(2)}) collective-permute-start(bf16[8,2,64,128]{3,2,1,0:T(8,128)(2,1)} %get-tuple-element.104), channel_id=1, source_target_pairs={{0,4},{1,5},{2,6},{3,7},{4,8},{5,9},{6,10},{7,11},{8,12},{9,13},{1... | collective-permute-start | bytes 786440 | tf_op jit(solution)/shard_map/ppermute | solution.py:582
  41.9 84.7 %collective-permute-start.4 = (bf16[8,2,64,128]{3,2,1,0:T(8,128)(2,1)}, bf16[8,2,64,128]{3,2,1,0:T(8,128)(2,1)S(1)}, u32[]{:S(2)}, u32[]{:S(2)}) collective-permute-start(bf16[8,2,64,128]{3,2,1,0:T(8,128)(2,1)} %get-tuple-element.105), channel_id=1, source_target_pairs={{0,5},{1,6},{2,7},{3,8},{4,9},{5,10},{6,11},{7,12},{8,13},{9,14},{... | collective-permute-start | bytes 786440 | tf_op jit(solution)/shard_map/ppermute | solution.py:582
  92.3 6.2 %copy-start.45 = (s32[1024]{0:T(1024)S(1)}, s32[1024]{0:T(1024)}, u32[]{:S(2)}) copy-start(s32[1024]{0:T(1024)} %param.10) | copy-start | bytes 12292
  93.8 147.8 %all-to-all-start.1 = ((bf16[16,4,2,64,128]{4,3,2,1,0:T(8,128)(2,1)}), bf16[16,4,2,64,128]{4,3,2,1,0:T(8,128)(2,1)S(1)}, u32[]{:S(2)}, u32[]{:S(2)}) async-start(bf16[16,4,2,64,128]{4,3,2,1,0:T(8,128)(2,1)} %channelise.5), calls=%async_computation.1 | async-start | bytes 4194304 | tf_op jit(solution)/shard_map/all_to_all | solution.py:587
  118.2 8.1 %copy-start.28 = (bf16[8,2,64,128]{3,2,1,0:T(8,128)(2,1)S(1)}, bf16[8,2,64,128]{3,2,1,0:T(8,128)(2,1)}, u32[]{:S(2)}) copy-start(bf16[8,2,64,128]{3,2,1,0:T(8,128)(2,1)} %get-tuple-element.109) | copy-start | bytes 786436
  118.2 8.5 %copy-start.27 = (bf16[8,2,64,128]{3,2,1,0:T(8,128)(2,1)S(1)}, bf16[8,2,64,128]{3,2,1,0:T(8,128)(2,1)}, u32[]{:S(2)}) copy-start(bf16[8,2,64,128]{3,2,1,0:T(8,128)(2,1)} %get-tuple-element.110) | copy-start | bytes 786436
  121.0 61.9 %copy-start.25 = (bf16[8,2,64,128]{3,2,1,0:T(8,128)(2,1)S(1)}, bf16[8,2,64,128]{3,2,1,0:T(8,128)(2,1)}, u32[]{:S(2)}) copy-start(bf16[8,2,64,128]{3,2,1,0:T(8,128)(2,1)} %get-tuple-element.111) | copy-start | bytes 786436
  121.1 67.5 %copy-start.23 = (bf16[8,2,64,128]{3,2,1,0:T(8,128)(2,1)S(1)}, bf16[8,2,64,128]{3,2,1,0:T(8,128)(2,1)}, u32[]{:S(2)}) copy-start(bf16[8,2,64,128]{3,2,1,0:T(8,128)(2,1)} %get-tuple-element.112) | copy-start | bytes 786436
  121.1 78.7 %copy-start.21 = (bf16[8,2,64,128]{3,2,1,0:T(8,128)(2,1)S(1)}, bf16[8,2,64,128]{3,2,1,0:T(8,128)(2,1)}, u32[]{:S(2)}) copy-start(bf16[8,2,64,128]{3,2,1,0:T(8,128)(2,1)} %get-tuple-element.113) | copy-start | bytes 786436
  121.1 78.7 %copy-start.19 = (bf16[8,2,64,128]{3,2,1,0:T(8,128)(2,1)S(1)}, bf16[8,2,64,128]{3,2,1,0:T(8,128)(2,1)}, u32[]{:S(2)}) copy-start(bf16[8,2,64,128]{3,2,1,0:T(8,128)(2,1)} %get-tuple-element.114) | copy-start | bytes 786436
  121.1 80.2 %copy-start.17 = (bf16[8,2,64,128]{3,2,1,0:T(8,128)(2,1)S(1)}, bf16[8,2,64,128]{3,2,1,0:T(8,128)(2,1)}, u32[]{:S(2)}) copy-start(bf16[8,2,64,128]{3,2,1,0:T(8,128)(2,1)} %get-tuple-element.115) | copy-start | bytes 786436
  121.1 11.3 %copy-start.18 = (bf16[8,2,64,128]{3,2,1,0:T(8,128)(2,1)}, bf16[8,2,64,128]{3,2,1,0:T(8,128)(2,1)S(1)}, u32[]{:S(2)}) copy-start(bf16[8,2,64,128]{3,2,1,0:T(8,128)(2,1)S(1)} %collective-permute-done.refs_1_) | copy-start | bytes 786436
  121.1 61.8 %collective-permute-start.5 = (bf16[8,2,64,128]{3,2,1,0:T(8,128)(2,1)S(1)}, bf16[8,2,64,128]{3,2,1,0:T(8,128)(2,1)S(1)}, u32[]{:S(2)}, u32[]{:S(2)}) collective-permute-start(bf16[8,2,64,128]{3,2,1,0:T(8,128)(2,1)S(1)} %copy-done.31), channel_id=1, source_target_pairs={{0,6},{1,7},{2,8},{3,9},{4,10},{5,11},{6,12},{7,13},{8,14},{9,15},... | collective-permute-start | bytes 786440 | tf_op jit(solution)/shard_map/ppermute | solution.py:582
  123.3 9.2 %copy-start.20 = (bf16[8,2,64,128]{3,2,1,0:T(8,128)(2,1)}, bf16[8,2,64,128]{3,2,1,0:T(8,128)(2,1)S(1)}, u32[]{:S(2)}) copy-start(bf16[8,2,64,128]{3,2,1,0:T(8,128)(2,1)S(1)} %collective-permute-done.1.refs_2_) | copy-start | bytes 786436
  123.3 65.3 %collective-permute-start.6 = (bf16[8,2,64,128]{3,2,1,0:T(8,128)(2,1)S(1)}, bf16[8,2,64,128]{3,2,1,0:T(8,128)(2,1)S(1)}, u32[]{:S(2)}, u32[]{:S(2)}) collective-permute-start(bf16[8,2,64,128]{3,2,1,0:T(8,128)(2,1)S(1)} %copy-done.30), channel_id=1, source_target_pairs={{0,7},{1,8},{2,9},{3,10},{4,11},{5,12},{6,13},{7,14},{8,15},{9,0},... | collective-permute-start | bytes 786440 | tf_op jit(solution)/shard_map/ppermute | solution.py:582
  124.2 8.3 %copy-start.22 = (bf16[8,2,64,128]{3,2,1,0:T(8,128)(2,1)}, bf16[8,2,64,128]{3,2,1,0:T(8,128)(2,1)S(1)}, u32[]{:S(2)}) copy-start(bf16[8,2,64,128]{3,2,1,0:T(8,128)(2,1)S(1)} %collective-permute-done.2.refs_3_) | copy-start | bytes 786436
  124.2 75.6 %collective-permute-start.7 = (bf16[8,2,64,128]{3,2,1,0:T(8,128)(2,1)S(1)}, bf16[8,2,64,128]{3,2,1,0:T(8,128)(2,1)S(1)}, u32[]{:S(2)}, u32[]{:S(2)}) collective-permute-start(bf16[8,2,64,128]{3,2,1,0:T(8,128)(2,1)S(1)} %copy-done.29), channel_id=1, source_target_pairs={{0,8},{1,9},{2,10},{3,11},{4,12},{5,13},{6,14},{7,15},{8,0},{9,1},... | collective-permute-start | bytes 786440 | tf_op jit(solution)/shard_map/ppermute | solution.py:582
  126.3 73.5 %collective-permute-start.8 = (bf16[8,2,64,128]{3,2,1,0:T(8,128)(2,1)S(1)}, bf16[8,2,64,128]{3,2,1,0:T(8,128)(2,1)S(1)}, u32[]{:S(2)}, u32[]{:S(2)}) collective-permute-start(bf16[8,2,64,128]{3,2,1,0:T(8,128)(2,1)S(1)} %copy-done.28), channel_id=1, source_target_pairs={{0,9},{1,10},{2,11},{3,12},{4,13},{5,14},{6,15},{7,0},{8,1},{9,2},... | collective-permute-start | bytes 786440 | tf_op jit(solution)/shard_map/ppermute | solution.py:582
  126.7 73.2 %collective-permute-start.9 = (bf16[8,2,64,128]{3,2,1,0:T(8,128)(2,1)S(1)}, bf16[8,2,64,128]{3,2,1,0:T(8,128)(2,1)S(1)}, u32[]{:S(2)}, u32[]{:S(2)}) collective-permute-start(bf16[8,2,64,128]{3,2,1,0:T(8,128)(2,1)S(1)} %copy-done.27), channel_id=1, source_target_pairs={{0,10},{1,11},{2,12},{3,13},{4,14},{5,15},{6,0},{7,1},{8,2},{9,3},... | collective-permute-start | bytes 786440 | tf_op jit(solution)/shard_map/ppermute | solution.py:582
  183.0 17.0 %copy-start.32 = (bf16[8,2,64,128]{3,2,1,0:T(8,128)(2,1)}, bf16[8,2,64,128]{3,2,1,0:T(8,128)(2,1)S(1)}, u32[]{:S(2)}) copy-start(bf16[8,2,64,128]{3,2,1,0:T(8,128)(2,1)S(1)} %collective-permute-done.5.refs_6_) | copy-start | bytes 786436
  183.0 32.5 %collective-permute-start.10 = (bf16[8,2,64,128]{3,2,1,0:T(8,128)(2,1)S(1)}, bf16[8,2,64,128]{3,2,1,0:T(8,128)(2,1)S(1)}, u32[]{:S(2)}, u32[]{:S(2)}) collective-permute-start(bf16[8,2,64,128]{3,2,1,0:T(8,128)(2,1)S(1)} %copy-done.25), channel_id=1, source_target_pairs={{0,11},{1,12},{2,13},{3,14},{4,15},{5,0},{6,1},{7,2},{8,3},{9,4},{... | collective-permute-start | bytes 786440 | tf_op jit(solution)/shard_map/ppermute | solution.py:582
  188.6 11.4 %copy-start.33 = (bf16[8,2,64,128]{3,2,1,0:T(8,128)(2,1)}, bf16[8,2,64,128]{3,2,1,0:T(8,128)(2,1)S(1)}, u32[]{:S(2)}) copy-start(bf16[8,2,64,128]{3,2,1,0:T(8,128)(2,1)S(1)} %collective-permute-done.6.refs_7_) | copy-start | bytes 786436
  188.6 26.9 %collective-permute-start.11 = (bf16[8,2,64,128]{3,2,1,0:T(8,128)(2,1)S(1)}, bf16[8,2,64,128]{3,2,1,0:T(8,128)(2,1)S(1)}, u32[]{:S(2)}, u32[]{:S(2)}) collective-permute-start(bf16[8,2,64,128]{3,2,1,0:T(8,128)(2,1)S(1)} %copy-done.23), channel_id=1, source_target_pairs={{0,12},{1,13},{2,14},{3,15},{4,0},{5,1},{6,2},{7,3},{8,4},{9,5},{1... | collective-permute-start | bytes 786440 | tf_op jit(solution)/shard_map/ppermute | solution.py:582
  199.8 15.7 %collective-permute-start.12 = (bf16[8,2,64,128]{3,2,1,0:T(8,128)(2,1)S(1)}, bf16[8,2,64,128]{3,2,1,0:T(8,128)(2,1)S(1)}, u32[]{:S(2)}, u32[]{:S(2)}) collective-permute-start(bf16[8,2,64,128]{3,2,1,0:T(8,128)(2,1)S(1)} %copy-done.21), channel_id=1, source_target_pairs={{0,13},{1,14},{2,15},{3,0},{4,1},{5,2},{6,3},{7,4},{8,5},{9,6},{10... | collective-permute-start | bytes 786440 | tf_op jit(solution)/shard_map/ppermute | solution.py:582
  199.8 21.4 %collective-permute-start.13 = (bf16[8,2,64,128]{3,2,1,0:T(8,128)(2,1)S(1)}, bf16[8,2,64,128]{3,2,1,0:T(8,128)(2,1)S(1)}, u32[]{:S(2)}, u32[]{:S(2)}) collective-permute-start(bf16[8,2,64,128]{3,2,1,0:T(8,128)(2,1)S(1)} %copy-done.19), channel_id=1, source_target_pairs={{0,14},{1,15},{2,0},{3,1},{4,2},{5,3},{6,4},{7,5},{8,6},{9,7},{10,... | collective-permute-start | bytes 786440 | tf_op jit(solution)/shard_map/ppermute | solution.py:582
  201.3 20.5 %collective-permute-start.14 = (bf16[8,2,64,128]{3,2,1,0:T(8,128)(2,1)S(1)}, bf16[8,2,64,128]{3,2,1,0:T(8,128)(2,1)S(1)}, u32[]{:S(2)}, u32[]{:S(2)}) collective-permute-start(bf16[8,2,64,128]{3,2,1,0:T(8,128)(2,1)S(1)} %copy-done.17), channel_id=1, source_target_pairs={{0,15},{1,0},{2,1},{3,2},{4,3},{5,4},{6,5},{7,6},{8,7},{9,8},{10,9... | collective-permute-start | bytes 786440 | tf_op jit(solution)/shard_map/ppermute | solution.py:582
  215.5 6.3 %copy-start.37 = (bf16[8,2,64,128]{3,2,1,0:T(8,128)(2,1)}, bf16[8,2,64,128]{3,2,1,0:T(8,128)(2,1)S(1)}, u32[]{:S(2)}) copy-start(bf16[8,2,64,128]{3,2,1,0:T(8,128)(2,1)S(1)} %collective-permute-done.10.refs_11_) | copy-start | bytes 786436
  215.5 6.3 %copy-start.38 = (bf16[8,2,64,128]{3,2,1,0:T(8,128)(2,1)}, bf16[8,2,64,128]{3,2,1,0:T(8,128)(2,1)S(1)}, u32[]{:S(2)}) copy-start(bf16[8,2,64,128]{3,2,1,0:T(8,128)(2,1)S(1)} %collective-permute-done.11.refs_12_) | copy-start | bytes 786436
  215.5 6.3 %copy-start.39 = (bf16[8,2,64,128]{3,2,1,0:T(8,128)(2,1)}, bf16[8,2,64,128]{3,2,1,0:T(8,128)(2,1)S(1)}, u32[]{:S(2)}) copy-start(bf16[8,2,64,128]{3,2,1,0:T(8,128)(2,1)S(1)} %collective-permute-done.12.refs_13_) | copy-start | bytes 786436
  249.7 13.0 %collective-permute-start.18 = (bf16[8,64,128]{2,1,0:T(8,128)(2,1)}, bf16[8,64,128]{2,1,0:T(8,128)(2,1)S(1)}, u32[]{:S(2)}, u32[]{:S(2)}) collective-permute-start(bf16[8,64,128]{2,1,0:T(8,128)(2,1)} %get-tuple-element.128), channel_id=1, source_target_pairs={{0,4},{1,5},{2,6},{3,7},{4,8},{5,9},{6,10},{7,11},{8,12},{9,13},{1... | collective-permute-start | bytes 393224 | tf_op jit(solution)/shard_map/ppermute | solution.py:582
  249.7 22.5 %collective-permute-start.19 = (bf16[8,64,128]{2,1,0:T(8,128)(2,1)}, bf16[8,64,128]{2,1,0:T(8,128)(2,1)S(1)}, u32[]{:S(2)}, u32[]{:S(2)}) collective-permute-start(bf16[8,64,128]{2,1,0:T(8,128)(2,1)} %get-tuple-element.129), channel_id=1, source_target_pairs={{0,5},{1,6},{2,7},{3,8},{4,9},{5,10},{6,11},{7,12},{8,13},{9,14},{... | collective-permute-start | bytes 393224 | tf_op jit(solution)/shard_map/ppermute | solution.py:582
  253.3 21.8 %collective-permute-start.20 = (bf16[8,64,128]{2,1,0:T(8,128)(2,1)}, bf16[8,64,128]{2,1,0:T(8,128)(2,1)S(1)}, u32[]{:S(2)}, u32[]{:S(2)}) collective-permute-start(bf16[8,64,128]{2,1,0:T(8,128)(2,1)} %get-tuple-element.130), channel_id=1, source_target_pairs={{0,6},{1,7},{2,8},{3,9},{4,10},{5,11},{6,12},{7,13},{8,14},{9,15},... | collective-permute-start | bytes 393224 | tf_op jit(solution)/shard_map/ppermute | solution.py:582
  253.3 24.7 %collective-permute-start.21 = (bf16[8,64,128]{2,1,0:T(8,128)(2,1)}, bf16[8,64,128]{2,1,0:T(8,128)(2,1)S(1)}, u32[]{:S(2)}, u32[]{:S(2)}) collective-permute-start(bf16[8,64,128]{2,1,0:T(8,128)(2,1)} %get-tuple-element.131), channel_id=1, source_target_pairs={{0,7},{1,8},{2,9},{3,10},{4,11},{5,12},{6,13},{7,14},{8,15},{9,0},... | collective-permute-start | bytes 393224 | tf_op jit(solution)/shard_map/ppermute | solution.py:582
  253.5 9.2 %copy-start.44 = (bf16[8,64,128]{2,1,0:T(8,128)(2,1)S(1)}, bf16[8,64,128]{2,1,0:T(8,128)(2,1)}, u32[]{:S(2)}) copy-start(bf16[8,64,128]{2,1,0:T(8,128)(2,1)} %get-tuple-element.133) | copy-start | bytes 393220
  253.5 18.7 %copy-start.43 = (bf16[8,64,128]{2,1,0:T(8,128)(2,1)S(1)}, bf16[8,64,128]{2,1,0:T(8,128)(2,1)}, u32[]{:S(2)}) copy-start(bf16[8,64,128]{2,1,0:T(8,128)(2,1)} %get-tuple-element.134) | copy-start | bytes 393220
  253.5 21.5 %copy-start.42 = (bf16[8,64,128]{2,1,0:T(8,128)(2,1)S(1)}, bf16[8,64,128]{2,1,0:T(8,128)(2,1)}, u32[]{:S(2)}) copy-start(bf16[8,64,128]{2,1,0:T(8,128)(2,1)} %get-tuple-element.135) | copy-start | bytes 393220
  253.5 30.0 %collective-permute-start.22 = (bf16[8,64,128]{2,1,0:T(8,128)(2,1)}, bf16[8,64,128]{2,1,0:T(8,128)(2,1)S(1)}, u32[]{:S(2)}, u32[]{:S(2)}) collective-permute-start(bf16[8,64,128]{2,1,0:T(8,128)(2,1)} %get-tuple-element.132), channel_id=1, source_target_pairs={{0,8},{1,9},{2,10},{3,11},{4,12},{5,13},{6,14},{7,15},{8,0},{9,1},... | collective-permute-start | bytes 393224 | tf_op jit(solution)/shard_map/ppermute | solution.py:582
  262.7 43.4 %copy-start.2 = (bf16[8,64,128]{2,1,0:T(8,128)(2,1)}, bf16[8,64,128]{2,1,0:T(8,128)(2,1)S(1)}, u32[]{:S(2)}) copy-start(bf16[8,64,128]{2,1,0:T(8,128)(2,1)S(1)} %collective-permute-done.18.refs_4_) | copy-start | bytes 393220
  262.8 20.8 %collective-permute-start.23 = (bf16[8,64,128]{2,1,0:T(8,128)(2,1)S(1)}, bf16[8,64,128]{2,1,0:T(8,128)(2,1)S(1)}, u32[]{:S(2)}, u32[]{:S(2)}) collective-permute-start(bf16[8,64,128]{2,1,0:T(8,128)(2,1)S(1)} %copy-done.44), channel_id=1, source_target_pairs={{0,9},{1,10},{2,11},{3,12},{4,13},{5,14},{6,15},{7,0},{8,1},{9,2},... | collective-permute-start | bytes 393224 | tf_op jit(solution)/shard_map/ppermute | solution.py:582
  272.3 33.9 %copy-start.3 = (bf16[8,64,128]{2,1,0:T(8,128)(2,1)}, bf16[8,64,128]{2,1,0:T(8,128)(2,1)S(1)}, u32[]{:S(2)}) copy-start(bf16[8,64,128]{2,1,0:T(8,128)(2,1)S(1)} %collective-permute-done.19.refs_5_) | copy-start | bytes 393220
  272.3 11.4 %collective-permute-start.24 = (bf16[8,64,128]{2,1,0:T(8,128)(2,1)S(1)}, bf16[8,64,128]{2,1,0:T(8,128)(2,1)S(1)}, u32[]{:S(2)}, u32[]{:S(2)}) collective-permute-start(bf16[8,64,128]{2,1,0:T(8,128)(2,1)S(1)} %copy-done.43), channel_id=1, source_target_pairs={{0,10},{1,11},{2,12},{3,13},{4,14},{5,15},{6,0},{7,1},{8,2},{9,3},... | collective-permute-start | bytes 393224 | tf_op jit(solution)/shard_map/ppermute | solution.py:582
  275.1 31.1 %copy-start.4 = (bf16[8,64,128]{2,1,0:T(8,128)(2,1)}, bf16[8,64,128]{2,1,0:T(8,128)(2,1)S(1)}, u32[]{:S(2)}) copy-start(bf16[8,64,128]{2,1,0:T(8,128)(2,1)S(1)} %collective-permute-done.20.refs_6_) | copy-start | bytes 393220
  275.1 11.7 %collective-permute-start.25 = (bf16[8,64,128]{2,1,0:T(8,128)(2,1)S(1)}, bf16[8,64,128]{2,1,0:T(8,128)(2,1)S(1)}, u32[]{:S(2)}, u32[]{:S(2)}) collective-permute-start(bf16[8,64,128]{2,1,0:T(8,128)(2,1)S(1)} %copy-done.42), channel_id=1, source_target_pairs={{0,11},{1,12},{2,13},{3,14},{4,15},{5,0},{6,1},{7,2},{8,3},{9,4},{... | collective-permute-start | bytes 393224 | tf_op jit(solution)/shard_map/ppermute | solution.py:582
  278.0 28.2 %copy-start.5 = (bf16[8,64,128]{2,1,0:T(8,128)(2,1)}, bf16[8,64,128]{2,1,0:T(8,128)(2,1)S(1)}, u32[]{:S(2)}) copy-start(bf16[8,64,128]{2,1,0:T(8,128)(2,1)S(1)} %collective-permute-done.21.refs_7_) | copy-start | bytes 393220
  278.0 9.0 %collective-permute-start.15 = (bf16[8,64,128]{2,1,0:T(8,128)(2,1)}, bf16[8,64,128]{2,1,0:T(8,128)(2,1)S(1)}, u32[]{:S(2)}, u32[]{:S(2)}) collective-permute-start(bf16[8,64,128]{2,1,0:T(8,128)(2,1)} %get-tuple-element.125), channel_id=1, source_target_pairs={{0,1},{1,2},{2,3},{3,4},{4,5},{5,6},{6,7},{7,8},{8,9},{9,10},{10,1... | collective-permute-start | bytes 393224 | tf_op jit(solution)/shard_map/ppermute | solution.py:582
  283.5 22.7 %copy-start.6 = (bf16[8,64,128]{2,1,0:T(8,128)(2,1)}, bf16[8,64,128]{2,1,0:T(8,128)(2,1)S(1)}, u32[]{:S(2)}) copy-start(bf16[8,64,128]{2,1,0:T(8,128)(2,1)S(1)} %collective-permute-done.22.refs_8_) | copy-start | bytes 393220
  283.5 11.5 %collective-permute-start.16 = (bf16[8,64,128]{2,1,0:T(8,128)(2,1)}, bf16[8,64,128]{2,1,0:T(8,128)(2,1)S(1)}, u32[]{:S(2)}, u32[]{:S(2)}) collective-permute-start(bf16[8,64,128]{2,1,0:T(8,128)(2,1)} %get-tuple-element.126), channel_id=1, source_target_pairs={{0,2},{1,3},{2,4},{3,5},{4,6},{5,7},{6,8},{7,9},{8,10},{9,11},{10,... | collective-permute-start | bytes 393224 | tf_op jit(solution)/shard_map/ppermute | solution.py:582
  283.5 22.7 %copy-start.7 = (bf16[8,64,128]{2,1,0:T(8,128)(2,1)}, bf16[8,64,128]{2,1,0:T(8,128)(2,1)S(1)}, u32[]{:S(2)}) copy-start(bf16[8,64,128]{2,1,0:T(8,128)(2,1)S(1)} %collective-permute-done.23.refs_9_) | copy-start | bytes 393220
  283.6 13.8 %collective-permute-start.17 = (bf16[8,64,128]{2,1,0:T(8,128)(2,1)}, bf16[8,64,128]{2,1,0:T(8,128)(2,1)S(1)}, u32[]{:S(2)}, u32[]{:S(2)}) collective-permute-start(bf16[8,64,128]{2,1,0:T(8,128)(2,1)} %get-tuple-element.127), channel_id=1, source_target_pairs={{0,3},{1,4},{2,5},{3,6},{4,7},{5,8},{6,9},{7,10},{8,11},{9,12},{10... | collective-permute-start | bytes 393224 | tf_op jit(solution)/shard_map/ppermute | solution.py:582
  283.6 22.6 %copy-start.8 = (bf16[8,64,128]{2,1,0:T(8,128)(2,1)}, bf16[8,64,128]{2,1,0:T(8,128)(2,1)S(1)}, u32[]{:S(2)}) copy-start(bf16[8,64,128]{2,1,0:T(8,128)(2,1)S(1)} %collective-permute-done.24.refs_10_) | copy-start | bytes 393220
  283.6 15.6 %collective-permute-start.26 = (bf16[8,64,128]{2,1,0:T(8,128)(2,1)}, bf16[8,64,128]{2,1,0:T(8,128)(2,1)S(1)}, u32[]{:S(2)}, u32[]{:S(2)}) collective-permute-start(bf16[8,64,128]{2,1,0:T(8,128)(2,1)} %get-tuple-element.136), channel_id=1, source_target_pairs={{0,12},{1,13},{2,14},{3,15},{4,0},{5,1},{6,2},{7,3},{8,4},{9,5},{1... | collective-permute-start | bytes 393224 | tf_op jit(solution)/shard_map/ppermute | solution.py:582
  286.8 19.5 %copy-start.9 = (bf16[8,64,128]{2,1,0:T(8,128)(2,1)}, bf16[8,64,128]{2,1,0:T(8,128)(2,1)S(1)}, u32[]{:S(2)}) copy-start(bf16[8,64,128]{2,1,0:T(8,128)(2,1)S(1)} %collective-permute-done.25.refs_11_) | copy-start | bytes 393220
  286.8 12.6 %collective-permute-start.27 = (bf16[8,64,128]{2,1,0:T(8,128)(2,1)}, bf16[8,64,128]{2,1,0:T(8,128)(2,1)S(1)}, u32[]{:S(2)}, u32[]{:S(2)}) collective-permute-start(bf16[8,64,128]{2,1,0:T(8,128)(2,1)} %get-tuple-element.137), channel_id=1, source_target_pairs={{0,13},{1,14},{2,15},{3,0},{4,1},{5,2},{6,3},{7,4},{8,5},{9,6},{10... | collective-permute-start | bytes 393224 | tf_op jit(solution)/shard_map/ppermute | solution.py:582
  286.9 19.3 %copy-start.10 = (bf16[8,64,128]{2,1,0:T(8,128)(2,1)}, bf16[8,64,128]{2,1,0:T(8,128)(2,1)S(1)}, u32[]{:S(2)}) copy-start(bf16[8,64,128]{2,1,0:T(8,128)(2,1)S(1)} %collective-permute-done.15.refs_1_) | copy-start | bytes 393220
  286.9 18.6 %collective-permute-start.28 = (bf16[8,64,128]{2,1,0:T(8,128)(2,1)}, bf16[8,64,128]{2,1,0:T(8,128)(2,1)S(1)}, u32[]{:S(2)}, u32[]{:S(2)}) collective-permute-start(bf16[8,64,128]{2,1,0:T(8,128)(2,1)} %get-tuple-element.138), channel_id=1, source_target_pairs={{0,14},{1,15},{2,0},{3,1},{4,2},{5,3},{6,4},{7,5},{8,6},{9,7},{10,... | collective-permute-start | bytes 393224 | tf_op jit(solution)/shard_map/ppermute | solution.py:582
  295.0 11.2 %copy-start.11 = (bf16[8,64,128]{2,1,0:T(8,128)(2,1)}, bf16[8,64,128]{2,1,0:T(8,128)(2,1)S(1)}, u32[]{:S(2)}) copy-start(bf16[8,64,128]{2,1,0:T(8,128)(2,1)S(1)} %collective-permute-done.16.refs_2_) | copy-start | bytes 393220
  295.0 11.2 %collective-permute-start.29 = (bf16[8,64,128]{2,1,0:T(8,128)(2,1)}, bf16[8,64,128]{2,1,0:T(8,128)(2,1)S(1)}, u32[]{:S(2)}, u32[]{:S(2)}) collective-permute-start(bf16[8,64,128]{2,1,0:T(8,128)(2,1)} %get-tuple-element.139), channel_id=1, source_target_pairs={{0,15},{1,0},{2,1},{3,2},{4,3},{5,4},{6,5},{7,6},{8,7},{9,8},{10,9... | collective-permute-start | bytes 393224 | tf_op jit(solution)/shard_map/ppermute | solution.py:582
  297.3 9.0 %copy-start.12 = (bf16[8,64,128]{2,1,0:T(8,128)(2,1)}, bf16[8,64,128]{2,1,0:T(8,128)(2,1)S(1)}, u32[]{:S(2)}) copy-start(bf16[8,64,128]{2,1,0:T(8,128)(2,1)S(1)} %collective-permute-done.17.refs_3_) | copy-start | bytes 393220
  299.3 7.0 %copy-start.13 = (bf16[8,64,128]{2,1,0:T(8,128)(2,1)}, bf16[8,64,128]{2,1,0:T(8,128)(2,1)S(1)}, u32[]{:S(2)}) copy-start(bf16[8,64,128]{2,1,0:T(8,128)(2,1)S(1)} %collective-permute-done.26.refs_12_) | copy-start | bytes 393220
  299.3 7.0 %copy-start.14 = (bf16[8,64,128]{2,1,0:T(8,128)(2,1)}, bf16[8,64,128]{2,1,0:T(8,128)(2,1)S(1)}, u32[]{:S(2)}) copy-start(bf16[8,64,128]{2,1,0:T(8,128)(2,1)S(1)} %collective-permute-done.27.refs_13_) | copy-start | bytes 393220
  (14 other events, 33.4 us)
